TPU v7x, 32 devices: a whole 2x2x4 slice. The times are simulated.
32 devices in a mesh: fsdp: 16 (over z, y, core), dp: 2 (over x).
Axes of the slice: x: 2, y: 2, z: 4, core: 2. Of those that a mesh axis runs over, the one named last changes fastest.
Arguments:
- tokens: bfloat16 [32768, 1024], P(('fsdp', 'dp')), may hold values from -6 to 6
- item_start: int32 [32768], P(('fsdp', 'dp')), may hold values from 0 to 896, as said below
- out_grad: bfloat16 [32768, 1024], P(('fsdp', 'dp')), may hold values from -6 to 6
- norm_gains: float32 [2, 1024], replicated, may hold values from 0.5 to 1.5
- norm_shifts: float32 [2, 1024], replicated, may hold values from -1.25 to 1.25
- w_qkv: bfloat16 [1024, 3072], P('fsdp'), may hold values from -0.1875 to 0.1875
- bias_qkv: float32 [3072], replicated, may hold values from -1.25 to 1.25
- w_out: bfloat16 [1024, 1024], P('fsdp'), may hold values from -0.5 to 0.5
- w_fc: bfloat16 [1024, 4096], P('fsdp'), may hold values from -0.1875 to 0.1875
- bias_fc: float32 [4096], replicated, may hold values from -1.75 to 1.75
- w_proj: bfloat16 [4096, 1024], P('fsdp'), may hold values from -0.09375 to 0.09375
- out_biases: float32 [2, 1024], replicated, may hold values from -1.25 to 1.25
- adapters: float32 [4, 1024, 4], replicated, may hold values from -0.3125 to 0.3125
- momentum: float32 [4, 1024, 4], replicated, may hold values from -1280 to 1280
- average: float32 [4, 1024, 4], replicated, may hold values from -0.3125 to 0.3125
Outputs:
- block_out: bfloat16 [32768, 1024], P(('fsdp', 'dp'))
- in_grad: float32 [32768, 1024], P(('fsdp', 'dp'))
- adapter_grad: float32 [4, 1024, 4], replicated
- new_momentum: float32 [4, 1024, 4], replicated
- new_adapters: float32 [4, 1024, 4], replicated
- new_average: float32 [4, 1024, 4], replicated
- adapter_copy: bfloat16 [4, 1024, 4], replicated
Inputs may be any that keep to these rules, and one draw needn't show every extreme that they name: `item_start`: each device's 1024 rows are cut into aligned runs of 1024 rows, and each run into items of 1024, 512, 256 or 128 rows at aligned places; every row holds the first row of its item, counted within its device. Every draw has an item of 1024 rows and one of 128 rows.
All inputs are finite; a program needn't handle non-finite values.
Results may differ from a plain program's by a relative error of at most 0.014.
The roundings to bfloat16 on the way count: a program that leaves them out, or rounds other values in their place, can miss the bound.
Values may be sent and summed in bfloat16 or wider, within the bound.
A program may use at most 256 MiB of HBM per device.

v0:
```python
import jax
import jax.numpy as jnp
from jax import lax
from jax.sharding import PartitionSpec as P

HEADS = 16


query_span = 512
adapter_scale = 8.0
score_scale = 0.125


def contract_trailing(left, right):
    return lax.dot_general(
        left, right, (((1,), (1,)), ((), ())), preferred_element_type=jnp.float32
    )


def contract_leading(left, right):
    return lax.dot_general(
        left, right, (((0,), (0,)), ((), ())), preferred_element_type=jnp.float32
    )


def layer_norm(values, gain, shift):
    center = values - jnp.mean(values, axis=-1, keepdims=True)
    spread = jnp.mean(center * center, axis=-1, keepdims=True)
    return center * lax.rsqrt(spread + 1e-05) * gain + shift


def gelu_tanh(values):
    return (
        0.5
        * values
        * (1.0 + jnp.tanh(0.7978845608 * (values + 0.044715 * values * values * values)))
    )


def block_scores(query_heads, key_heads, starts, block_index, span_rows):
    row_count = key_heads.shape[0]
    begin_row = block_index * span_rows
    query_block = lax.dynamic_slice_in_dim(query_heads, begin_row, span_rows, 0)
    start_block = lax.dynamic_slice_in_dim(starts, begin_row, span_rows, 0)
    columns = jnp.arange(row_count, dtype=jnp.int32)
    row_ids = begin_row + jnp.arange(span_rows, dtype=jnp.int32)
    scores = (
        jnp.einsum("qhe,khe->hqk", query_block, key_heads, preferred_element_type=jnp.float32)
        * score_scale
    )
    visible = (start_block[:, None] <= columns[None, :]) & (columns[None, :] <= row_ids[:, None])
    return (query_block, jnp.where(visible[None], scores, jnp.float32(-1e30)))


def attend_forward(query_heads, key_heads, value_heads, starts):
    row_count = query_heads.shape[0]
    span_rows = min(query_span, row_count)

    def one_block(block_index):
        query_block, scores = block_scores(query_heads, key_heads, starts, block_index, span_rows)
        highest = jnp.max(scores, axis=-1, keepdims=True)
        raised = jnp.exp(scores - highest)
        totals = jnp.sum(raised, axis=-1, keepdims=True)
        probs = raised / totals
        result = jnp.einsum(
            "hqk,khe->qhe",
            probs.astype(jnp.bfloat16),
            value_heads,
            preferred_element_type=jnp.float32,
        )
        return (result.astype(jnp.bfloat16), (highest + jnp.log(totals))[..., 0])

    outputs, log_sums = lax.map(one_block, jnp.arange(row_count // span_rows, dtype=jnp.int32))
    return (outputs.reshape(query_heads.shape), log_sums)


def attend_backward(query_heads, key_heads, value_heads, grad_heads, log_sums, starts):
    row_count = query_heads.shape[0]
    span_rows = min(query_span, row_count)

    def one_block(carry, block_index):
        grad_keys, value_gradient = carry
        query_block, scores = block_scores(query_heads, key_heads, starts, block_index, span_rows)
        grad_block = lax.dynamic_slice_in_dim(grad_heads, block_index * span_rows, span_rows, 0)
        probs = jnp.exp(scores - log_sums[block_index][:, :, None])
        grad_probs = jnp.einsum(
            "qhe,khe->hqk", grad_block, value_heads, preferred_element_type=jnp.float32
        )
        value_gradient = value_gradient + jnp.einsum(
            "hqk,qhe->khe",
            probs.astype(jnp.bfloat16),
            grad_block,
            preferred_element_type=jnp.float32,
        )
        inner = jnp.sum(probs * grad_probs, axis=-1, keepdims=True)
        grad_scores = (probs * (grad_probs - inner)).astype(jnp.bfloat16)
        query_gradient = (
            jnp.einsum("hqk,khe->qhe", grad_scores, key_heads, preferred_element_type=jnp.float32)
            * score_scale
        )
        grad_keys = (
            grad_keys
            + jnp.einsum(
                "hqk,qhe->khe", grad_scores, query_block, preferred_element_type=jnp.float32
            )
            * score_scale
        )
        return ((grad_keys, value_gradient), query_gradient.astype(jnp.bfloat16))

    zeros_heads = jnp.zeros(key_heads.shape, jnp.float32)
    (grad_keys, value_gradient), grad_queries = lax.scan(
        one_block, (zeros_heads, zeros_heads), jnp.arange(row_count // span_rows, dtype=jnp.int32)
    )
    return (
        grad_queries.reshape(query_heads.shape),
        grad_keys.astype(jnp.bfloat16),
        value_gradient.astype(jnp.bfloat16),
    )


def per_device(
    tokens,
    item_start,
    out_grad,
    norm_gains,
    norm_shifts,
    w_qkv,
    bias_qkv,
    w_out,
    w_fc,
    bias_fc,
    w_proj,
    out_biases,
    adapters,
    momentum,
    average,
):
    row_count, hidden_width = tokens.shape
    head_size = hidden_width // HEADS
    qkv_full, out_full = (
        lax.all_gather(w_qkv, "fsdp", axis=0, tiled=True),
        lax.all_gather(w_out, "fsdp", axis=0, tiled=True),
    )
    fc_full, proj_full = (
        lax.all_gather(w_fc, "fsdp", axis=0, tiled=True),
        lax.all_gather(w_proj, "fsdp", axis=0, tiled=True),
    )
    reduced_adapter_pass = adapters.astype(jnp.bfloat16)
    residual = tokens.astype(jnp.float32)

    def norm_first(values):
        return layer_norm(values, norm_gains[0], norm_shifts[0])

    def norm_second(values):
        return layer_norm(values, norm_gains[1], norm_shifts[1])

    normed_one, back_first = jax.vjp(norm_first, residual)
    normed_one = normed_one.astype(jnp.bfloat16)
    mixed_tokens_full = jnp.dot(normed_one, qkv_full, preferred_element_type=jnp.float32) + bias_qkv
    query_down_matrix = jnp.dot(
        normed_one, reduced_adapter_pass[0], preferred_element_type=jnp.float32
    ).astype(jnp.bfloat16)
    value_down_matrix = jnp.dot(
        normed_one, reduced_adapter_pass[2], preferred_element_type=jnp.float32
    ).astype(jnp.bfloat16)
    query_rows = (
        mixed_tokens_full[:, :hidden_width]
        + adapter_scale * contract_trailing(query_down_matrix, reduced_adapter_pass[1])
    ).astype(jnp.bfloat16)
    keys_all = mixed_tokens_full[:, hidden_width : 2 * hidden_width].astype(jnp.bfloat16)
    value_rows_full = (
        mixed_tokens_full[:, 2 * hidden_width :]
        + adapter_scale * contract_trailing(value_down_matrix, reduced_adapter_pass[3])
    ).astype(jnp.bfloat16)
    heads_shape = (row_count, HEADS, head_size)
    query_heads = query_rows.reshape(heads_shape)
    key_heads = keys_all.reshape(heads_shape)
    value_heads = value_rows_full.reshape(heads_shape)
    attended, log_sums = attend_forward(query_heads, key_heads, value_heads, item_start)
    attended = attended.reshape(row_count, hidden_width)
    middle = (
        residual + jnp.dot(attended, out_full, preferred_element_type=jnp.float32) + out_biases[0]
    )
    normed_two, back_second = jax.vjp(norm_second, middle)
    normed_two = normed_two.astype(jnp.bfloat16)
    pre_act = jnp.dot(normed_two, fc_full, preferred_element_type=jnp.float32) + bias_fc
    activation, back_gelu = jax.vjp(gelu_tanh, pre_act)
    activation = activation.astype(jnp.bfloat16)
    result = (
        middle + jnp.dot(activation, proj_full, preferred_element_type=jnp.float32) + out_biases[1]
    )
    block_out = result.astype(jnp.bfloat16)
    fc_back, proj_back = (
        lax.all_gather(w_fc, "fsdp", axis=0, tiled=True),
        lax.all_gather(w_proj, "fsdp", axis=0, tiled=True),
    )
    qkv_back, out_back = (
        lax.all_gather(w_qkv, "fsdp", axis=0, tiled=True),
        lax.all_gather(w_out, "fsdp", axis=0, tiled=True),
    )
    grad_act = contract_trailing(out_grad, proj_back)
    grad_pre = back_gelu(grad_act)[0].astype(jnp.bfloat16)
    grad_norm_two = contract_trailing(grad_pre, fc_back)
    grad_middle = out_grad.astype(jnp.float32) + back_second(grad_norm_two)[0]
    grad_branch = grad_middle.astype(jnp.bfloat16)
    grad_attended = (
        contract_trailing(grad_branch, out_back).astype(jnp.bfloat16).reshape(heads_shape)
    )
    query_gradient, grad_keys, value_gradient = attend_backward(
        query_heads, key_heads, value_heads, grad_attended, log_sums, item_start
    )
    query_gradient = query_gradient.reshape(row_count, hidden_width)
    grad_keys = grad_keys.reshape(row_count, hidden_width)
    value_gradient = value_gradient.reshape(row_count, hidden_width)
    grad_mixed = jnp.concatenate([query_gradient, grad_keys, value_gradient], axis=1)
    grad_down_q = (
        adapter_scale
        * jnp.dot(query_gradient, reduced_adapter_pass[1], preferred_element_type=jnp.float32)
    ).astype(jnp.bfloat16)
    grad_down_v = (
        adapter_scale
        * jnp.dot(value_gradient, reduced_adapter_pass[3], preferred_element_type=jnp.float32)
    ).astype(jnp.bfloat16)
    grad_norm_one = (
        contract_trailing(grad_mixed, qkv_back)
        + contract_trailing(grad_down_q, reduced_adapter_pass[0])
        + contract_trailing(grad_down_v, reduced_adapter_pass[2])
    )
    in_grad = grad_middle + back_first(grad_norm_one)[0]
    local_grads = jnp.stack(
        [
            contract_leading(normed_one, grad_down_q),
            adapter_scale * contract_leading(query_gradient, query_down_matrix),
            contract_leading(normed_one, grad_down_v),
            adapter_scale * contract_leading(value_gradient, value_down_matrix),
        ]
    )
    adapter_grad = lax.psum(local_grads, ("fsdp", "dp"))
    tokens_total = row_count * lax.axis_size("fsdp") * lax.axis_size("dp")
    step_rate = 0.01 / jnp.sqrt(jnp.float32(tokens_total))
    new_momentum = 0.9 * momentum + adapter_grad
    new_adapters = adapters - step_rate * (adapter_grad + 0.9 * new_momentum)
    new_average = 0.9 * average + 0.1 * new_adapters
    return (
        block_out,
        in_grad,
        adapter_grad,
        new_momentum,
        new_adapters,
        new_average,
        new_adapters.astype(jnp.bfloat16),
    )


def solution(mesh):
    in_specs = (
        P(("fsdp", "dp"), None),
        P(("fsdp", "dp")),
        P(("fsdp", "dp"), None),
        P(),
        P(),
        P("fsdp", None),
        P(),
        P("fsdp", None),
        P("fsdp", None),
        P(),
        P("fsdp", None),
        P(),
        P(),
        P(),
        P(),
    )
    out_specs = (P(("fsdp", "dp"), None), P(("fsdp", "dp"), None), P(), P(), P(), P(), P())
    return jax.shard_map(
        per_device, mesh=mesh, in_specs=in_specs, out_specs=out_specs, check_vma=False
    )
```

profile of v0, /device:TPU:0, one launch (start us, length us, event | category | flops | bytes accessed | tf_op | source)
XLA Modules:
  0.0 686.4 jit_solution(17003402721910862022)
XLA Ops:
  23.1 51.8 %all-gather.5.cloned.1.call-done = bf16[1024,3072]{1,0:T(8,128)(2,1)} async-done(((bf16[64,3072]{1,0:T(8,128)(2,1)}), bf16[1024,3072]{1,0:T(8,128)(2,1)}) %all-gather.5.cloned.1.call-update) | async-done | bytes 6291472 | tf_op jit(solution)/shard_map/all_gather | solution.py:141
  105.0 100.5 %while.27 = (s32[]{:T(128)}, bf16[2,512,16,64]{1,3,2,0:T(8,128)(2,1)}, f32[2,16,512]{2,1,0:T(8,128)S(1)}, s32[2]{0:T(128)S(1)}, s32[1024]{0:T(1024)}, /*index=5*...) while((s32[]{:T(128)}, ...), condition=%wide.region_5.6_spmd, body=%wide.region_2.5_spmd.sunk | while | flops 2250236416 | bytes 134490384 | solution.py:73
  107.8 15.4 %fusion.152 = (f32[16,512]{1,0:T(8,128)S(1)}, f32[16,512,1024]{2,1,0:T(8,128)}) fusion(pred[512,1024]{1,0:T(8,128)(4,1)S(1)} %fusion.151, bf16[1024,16,64]{0,2,1:T(8,128)(2,1)S(1)} %get-tuple-element.396, bf16[1024,16,64]{0,2,1:T(8,128)(2,1)} %get-tuple-element.395, s32[]{:T(128)S(6)} %select_n.60), kind=kOutput, calls=%fused_computation.3.clone.1 | convolution fusion | flops 1098899456 | bytes 37257220 | tf_op jit(solution)/shard_map/while/body/eval_jaxpr/qhe,khe->hqk/dot_general | solution.py:48
  123.2 15.9 %fusion.153 = f32[16,512]{1,0:T(8,128)S(1)} fusion(f32[16,512,1024]{2,1,0:T(8,128)} %get-tuple-element.351, f32[16,512]{1,0:T(8,128)S(1)} %get-tuple-element.352, pred[512,1024]{1,0:T(8,128)(4,1)S(1)} %fusion.151), kind=kLoop, calls=%fused_computation.4.clone.1 | loop fusion | flops 33546240 | bytes 34144256 | tf_op jit(solution)/shard_map/while/body/eval_jaxpr/reduce_sum | solution.py:63
  139.1 14.7 %fusion.154 = bf16[2,512,16,64]{1,3,2,0:T(8,128)(2,1)S(1)} fusion(bf16[2,512,16,64]{1,3,2,0:T(8,128)(2,1)S(1)} %copy-done.12, s32[]{:T(128)S(6)} %copy.58, bf16[1024,16,64]{0,2,1:T(8,128)(2,1)S(1)} %copy-done.1, f32[16,512,1024]{2,1,0:T(8,128)} %get-tuple-element.351, f32[16,512]{1,0:T(8,128)S(1)} %fusion.153, ...), kind=kOutput, calls=%fused_computation.11.clone.1 | convolution fusion | flops 1116209152 | bytes 37289988 | tf_op jit(solution)/shard_map/while/body/eval_jaxpr/hqk,khe->qhe/dot_general | solution.py:65
  157.7 15.5 %fusion.152 = (f32[16,512]{1,0:T(8,128)S(1)}, f32[16,512,1024]{2,1,0:T(8,128)}) fusion(pred[512,1024]{1,0:T(8,128)(4,1)S(1)} %fusion.151, bf16[1024,16,64]{0,2,1:T(8,128)(2,1)S(1)} %get-tuple-element.396, bf16[1024,16,64]{0,2,1:T(8,128)(2,1)} %get-tuple-element.395, s32[]{:T(128)S(6)} %select_n.60), kind=kOutput, calls=%fused_computation.3.clone.1 | convolution fusion | flops 1098899456 | bytes 37257220 | tf_op jit(solution)/shard_map/while/body/eval_jaxpr/qhe,khe->hqk/dot_general | solution.py:48
  173.2 15.7 %fusion.153 = f32[16,512]{1,0:T(8,128)S(1)} fusion(f32[16,512,1024]{2,1,0:T(8,128)} %get-tuple-element.351, f32[16,512]{1,0:T(8,128)S(1)} %get-tuple-element.352, pred[512,1024]{1,0:T(8,128)(4,1)S(1)} %fusion.151), kind=kLoop, calls=%fused_computation.4.clone.1 | loop fusion | flops 33546240 | bytes 34144256 | tf_op jit(solution)/shard_map/while/body/eval_jaxpr/reduce_sum | solution.py:63
  188.9 14.9 %fusion.154 = bf16[2,512,16,64]{1,3,2,0:T(8,128)(2,1)S(1)} fusion(bf16[2,512,16,64]{1,3,2,0:T(8,128)(2,1)S(1)} %copy-done.12, s32[]{:T(128)S(6)} %copy.58, bf16[1024,16,64]{0,2,1:T(8,128)(2,1)S(1)} %copy-done.1, f32[16,512,1024]{2,1,0:T(8,128)} %get-tuple-element.351, f32[16,512]{1,0:T(8,128)S(1)} %fusion.153, ...), kind=kOutput, calls=%fused_computation.11.clone.1 | convolution fusion | flops 1116209152 | bytes 37289988 | tf_op jit(solution)/shard_map/while/body/eval_jaxpr/hqk,khe->qhe/dot_general | solution.py:65
  219.5 16.9 %fusion.63 = f32[1024,4096]{1,0:T(8,128)} fusion(bf16[1024,4096]{1,0:T(8,128)(2,1)} %all-gather.9.cloned.1.call-done, f32[1024,1024]{0,1:T(8,128)} %copy-done.8, f32[1024]{0:T(1024)S(1)} %bitcast.155, f32[1024]{0:T(1024)S(1)} %bitcast.150, f32[1024]{0:T(1024)S(1)} %fusion.79, f32[1024]{0:T(1024)S(1)} %broadcast_multiply_fusion), kind=kOutput, calls=%fused_computation.96 | convolution fusion | flops 8595177472 | bytes 29376512 | tf_op jit(solution)/shard_map/dot_general | solution.py:186
  236.3 31.9 %all-gather.11.cloned.1.call-done = bf16[4096,1024]{1,0:T(8,128)(2,1)} async-done(((bf16[256,1024]{1,0:T(8,128)(2,1)}), bf16[4096,1024]{1,0:T(8,128)(2,1)}) %all-gather.11.cloned.1.call-update) | async-done | bytes 8388624 | tf_op jit(solution)/shard_map/all_gather | solution.py:146
  268.2 33.6 %multiply_reduce_fusion.1 = (f32[1024]{0:T(1024)S(1)}, f32[1024,1024]{0,1:T(8,128)}) fusion(f32[1024,1024]{0,1:T(8,128)} %copy-done.8, f32[1024]{0:T(1024)S(1)} %bitcast.151, f32[1024]{0:T(1024)S(1)} %broadcast_multiply_fusion, bf16[1024,4096]{1,0:T(8,128)(2,1)} %all-gather.9.cloned.1.call-done, f32[1024,4096]{1,0:T(8,128)} %fusion.63, ...), kind=kOutput, calls=%fused_computation.90 | convolution fusion | flops 17288921088 | bytes 44068864 | tf_op jit(solution)/shard_map/dot_general | solution.py:15
  311.9 224.7 %while.28 = (s32[]{:T(128)}, f32[1024,16,64]{0,2,1:T(8,128)}, f32[1024,16,64]{0,2,1:T(8,128)}, bf16[2,512,16,64]{1,3,2,0:T(8,128)(2,1)}, s32[2]{0:T(128)S(1)}, /...) while((s32[]{:T(128)}, f32[1024,16,64]{0,2,1:T(8,128)}, ...), condition=%wide.region_12.13_spmd.clone, body=%wide.region_10.12_spmd.clone.sunk | while | flops 5502394880 | bytes 282831200 | solution.py:111
  313.5 14.4 %fusion.164 = f32[16,512,1024]{2,1,0:T(8,128)} fusion(bf16[1024,16,64]{0,2,1:T(8,128)(2,1)S(1)} %get-tuple-element.441, bf16[1024,16,64]{0,2,1:T(8,128)(2,1)} %get-tuple-element.439, s32[]{:T(128)S(6)} %select_n.64), kind=kOutput, calls=%fused_computation.37.clone.1 | convolution fusion | flops 1073741824 | bytes 36700164 | tf_op jit(solution)/shard_map/while/body/eval_jaxpr/qhe,khe->hqk/dot_general | solution.py:48
  331.0 26.0 %multiply_reduce_fusion.4 = (f32[16,512]{1,0:T(8,128)S(1)}, f32[16,512,1024]{2,1,0:T(8,128)}) fusion(f32[16,512,1024]{2,1,0:T(8,128)} %fusion.164, f32[16,512]{1,0:T(8,128)S(1)} %dynamic-slice_bitcast_fusion.2, pred[512,1024]{1,0:T(8,128)(4,1)S(1)} %fusion.165, bf16[1024,16,64]{0,2,1:T(8,128)(2,1)} %get-tuple-element.444, ...), kind=kOutput, calls=%fused_computation.20.clone.1 | convolution fusion | flops 1115676672 | bytes 70844416 | tf_op jit(solution)/shard_map/while/body/eval_jaxpr/qhe,khe->hqk/dot_general | solution.py:86
  357.0 27.8 %multiply_convert_fusion.7 = bf16[16,512,1024]{2,1,0:T(8,128)(2,1)} fusion(f32[16,512,1024]{2,1,0:T(8,128)} %get-tuple-element.364, f32[16,512,1024]{2,1,0:T(8,128)} %fusion.164, f32[16,512]{1,0:T(8,128)S(1)} %get-tuple-element.365, f32[16,512]{1,0:T(8,128)S(1)} %dynamic-slice_bitcast_fusion.2, pred[512,1024]{1,0:T(8,128)(4,1)S(1)} %fusion.165), kind=kLoop, calls=%fused_computation.19.clone.1 | loop fusion | flops 50331648 | bytes 84475904 | tf_op jit(solution)/shard_map/while/body/eval_jaxpr/convert_element_type | solution.py:96
  384.8 11.1 %bitcast_add_fusion.4 = f32[1024,16,64]{0,2,1:T(8,128)} fusion(f32[1024,16,64]{0,2,1:T(8,128)} %get-tuple-element.419, bf16[16,512,1024]{2,1,0:T(8,128)(2,1)} %multiply_convert_fusion.7, pred[]{:T(512)S(6)} %compare.3, bf16[1024,16,64]{0,2,1:T(8,128)(2,1)} %get-tuple-element.439, s32[]{:T(128)S(6)} %select_n.64), kind=kOutput, calls=%fused_computation.26.clone.1 | convolution fusion | flops 1076887552 | bytes 26214404 | tf_op jit(solution)/shard_map/while/body/eval_jaxpr/hqk,qhe->khe/dot_general | solution.py:103
  395.9 17.5 %bitcast_add_fusion.5 = f32[1024,16,64]{0,2,1:T(8,128)} fusion(f32[1024,16,64]{0,2,1:T(8,128)} %get-tuple-element.420, f32[16,512,1024]{2,1,0:T(8,128)} %fusion.164, f32[16,512]{1,0:T(8,128)S(1)} %dynamic-slice_bitcast_fusion.2, pred[512,1024]{1,0:T(8,128)(4,1)S(1)} %fusion.165, pred[]{:T(512)S(6)} %compare.3, ...), kind=kOutput, calls=%fused_computation.25.clone.1 | convolution fusion | flops 1109393408 | bytes 43548676 | tf_op jit(solution)/shard_map/while/body/eval_jaxpr/hqk,qhe->khe/dot_general | solution.py:89
  424.4 14.4 %fusion.164 = f32[16,512,1024]{2,1,0:T(8,128)} fusion(bf16[1024,16,64]{0,2,1:T(8,128)(2,1)S(1)} %get-tuple-element.441, bf16[1024,16,64]{0,2,1:T(8,128)(2,1)} %get-tuple-element.439, s32[]{:T(128)S(6)} %select_n.64), kind=kOutput, calls=%fused_computation.37.clone.1 | convolution fusion | flops 1073741824 | bytes 36700164 | tf_op jit(solution)/shard_map/while/body/eval_jaxpr/qhe,khe->hqk/dot_general | solution.py:48
  441.9 26.0 %multiply_reduce_fusion.4 = (f32[16,512]{1,0:T(8,128)S(1)}, f32[16,512,1024]{2,1,0:T(8,128)}) fusion(f32[16,512,1024]{2,1,0:T(8,128)} %fusion.164, f32[16,512]{1,0:T(8,128)S(1)} %dynamic-slice_bitcast_fusion.2, pred[512,1024]{1,0:T(8,128)(4,1)S(1)} %fusion.165, bf16[1024,16,64]{0,2,1:T(8,128)(2,1)} %get-tuple-element.444, ...), kind=kOutput, calls=%fused_computation.20.clone.1 | convolution fusion | flops 1115676672 | bytes 70844416 | tf_op jit(solution)/shard_map/while/body/eval_jaxpr/qhe,khe->hqk/dot_general | solution.py:86
  467.9 27.8 %multiply_convert_fusion.7 = bf16[16,512,1024]{2,1,0:T(8,128)(2,1)} fusion(f32[16,512,1024]{2,1,0:T(8,128)} %get-tuple-element.364, f32[16,512,1024]{2,1,0:T(8,128)} %fusion.164, f32[16,512]{1,0:T(8,128)S(1)} %get-tuple-element.365, f32[16,512]{1,0:T(8,128)S(1)} %dynamic-slice_bitcast_fusion.2, pred[512,1024]{1,0:T(8,128)(4,1)S(1)} %fusion.165), kind=kLoop, calls=%fused_computation.19.clone.1 | loop fusion | flops 50331648 | bytes 84475904 | tf_op jit(solution)/shard_map/while/body/eval_jaxpr/convert_element_type | solution.py:96
  495.7 12.3 %bitcast_add_fusion.4 = f32[1024,16,64]{0,2,1:T(8,128)} fusion(f32[1024,16,64]{0,2,1:T(8,128)} %get-tuple-element.419, bf16[16,512,1024]{2,1,0:T(8,128)(2,1)} %multiply_convert_fusion.7, pred[]{:T(512)S(6)} %compare.3, bf16[1024,16,64]{0,2,1:T(8,128)(2,1)} %get-tuple-element.439, s32[]{:T(128)S(6)} %select_n.64), kind=kOutput, calls=%fused_computation.26.clone.1 | convolution fusion | flops 1076887552 | bytes 26214404 | tf_op jit(solution)/shard_map/while/body/eval_jaxpr/hqk,qhe->khe/dot_general | solution.py:103
  508.0 18.7 %bitcast_add_fusion.5 = f32[1024,16,64]{0,2,1:T(8,128)} fusion(f32[1024,16,64]{0,2,1:T(8,128)} %get-tuple-element.420, f32[16,512,1024]{2,1,0:T(8,128)} %fusion.164, f32[16,512]{1,0:T(8,128)S(1)} %dynamic-slice_bitcast_fusion.2, pred[512,1024]{1,0:T(8,128)(4,1)S(1)} %fusion.165, pred[]{:T(512)S(6)} %compare.3, ...), kind=kOutput, calls=%fused_computation.25.clone.1 | convolution fusion | flops 1109393408 | bytes 43548676 | tf_op jit(solution)/shard_map/while/body/eval_jaxpr/hqk,qhe->khe/dot_general | solution.py:89
  560.1 17.0 %add_convert_fusion = bf16[1024,1024]{0,1:T(8,128)(2,1)} fusion(f32[1024,1024]{0,1:T(8,128)} %copy-done.8, f32[1024]{0:T(1024)S(1)} %bitcast.154, bf16[4096,1024]{1,0:T(8,128)(2,1)} %all-gather.11.cloned.1.call-done, f32[1024,4096]{1,0:T(8,128)} %fusion.63, f32[4096]{0:T(1024)S(1)} %copy-done.47), kind=kOutput, calls=%fused_computation.91 | convolution fusion | flops 8635023360 | bytes 31477760 | tf_op jit(solution)/shard_map/dot_general | solution.py:190
  594.2 81.9 %all-reduce.2.cloned.1.call-done = f32[4,1024,4]{1,2,0:T(4,128)} async-done(((f32[4,1024,4]{1,2,0:T(4,128)}), f32[4,1024,4]{1,2,0:T(4,128)}) %all-reduce.2.cloned.1.call-update) | async-done | bytes 65552 | tf_op jit(solution)/shard_map/psum | solution.py:238
  (207 shorter events, 143.7 us)
Async XLA Ops:
  7.2 67.7 %all-gather.5.cloned.1.call-start = ((), (), s32[]{:S(2)}) async-start(), calls=%async_computation | async-start | bytes 6684672 | tf_op jit(solution)/shard_map/all_gather | solution.py:141
  7.9 203.3 %all-gather.7.cloned.1.call-start = ((), (), s32[]{:S(2)}) async-start(), calls=%async_computation.1 | async-start | bytes 2228224 | tf_op jit(solution)/shard_map/all_gather | solution.py:142
  8.7 210.8 %all-gather.9.cloned.1.call-start = ((), (), s32[]{:S(2)}) async-start(), calls=%async_computation.2 | async-start | bytes 8912896 | tf_op jit(solution)/shard_map/all_gather | solution.py:145
  9.4 258.8 %all-gather.11.cloned.1.call-start = ((), (), s32[]{:S(2)}) async-start(), calls=%async_computation.3 | async-start | bytes 8912896 | tf_op jit(solution)/shard_map/all_gather | solution.py:146
  10.0 666.0 %all-reduce.2.cloned.1.call-start = ((), (), s32[]{:S(2)}) async-start(), calls=%async_computation.4 | async-start | bytes 131072 | tf_op jit(solution)/shard_map/psum | solution.py:238
  15.9 79.4 %copy-start.17 = (bf16[4,1024,4]{1,2,0:T(4,128)(2,1)}, bf16[4,1024,4]{1,2,0:T(4,128)(2,1)S(1)}, u32[]{:S(2)}) copy-start(bf16[4,1024,4]{1,2,0:T(4,128)(2,1)S(1)} %convert_element_type.81) | copy-start | bytes 98308
  16.7 58.2 %copy-start.48 = (f32[3072]{0:T(1024)S(1)}, f32[3072]{0:T(1024)}, u32[]{:S(2)}) copy-start(f32[3072]{0:T(1024)} %param.25) | copy-start | bytes 36868
  18.0 67.7 %copy-start.24 = (bf16[1024,4]{0,1:T(4,128)(2,1)}, bf16[1024,4]{0,1:T(4,128)(2,1)S(1)}, u32[]{:S(2)}) copy-start(bf16[1024,4]{0,1:T(4,128)(2,1)S(1)} %convolution_convert_fusion.1) | copy-start | bytes 24580
  18.4 76.8 %copy-start.26 = (bf16[1024,4]{0,1:T(4,128)(2,1)}, bf16[1024,4]{0,1:T(4,128)(2,1)S(1)}, u32[]{:S(2)}) copy-start(bf16[1024,4]{0,1:T(4,128)(2,1)S(1)} %convolution_convert_fusion) | copy-start | bytes 24580
  18.4 56.5 %copy-start.5 = (bf16[1024,1024]{0,1:T(8,128)(2,1)S(1)}, bf16[1024,1024]{0,1:T(8,128)(2,1)}, u32[]{:S(2)}) copy-start(bf16[1024,1024]{0,1:T(8,128)(2,1)} %copy-done.4) | copy-start | bytes 6291460
  123.2 15.9 %copy-start.1 = (bf16[1024,16,64]{0,2,1:T(8,128)(2,1)S(1)}, bf16[1024,16,64]{0,2,1:T(8,128)(2,1)}, u32[]{:S(2)}) copy-start(bf16[1024,16,64]{0,2,1:T(8,128)(2,1)} %get-tuple-element.397) | copy-start | bytes 6291460 | tf_op jit(solution)/shard_map/while
  123.2 15.9 %copy-start.12 = (bf16[2,512,16,64]{1,3,2,0:T(8,128)(2,1)S(1)}, bf16[2,512,16,64]{1,3,2,0:T(8,128)(2,1)}, u32[]{:S(2)}) copy-start(bf16[2,512,16,64]{1,3,2,0:T(8,128)(2,1)} %get-tuple-element.379) | copy-start | bytes 6291460 | tf_op jit(solution)/shard_map/while
  173.2 15.7 %copy-start.1 = (bf16[1024,16,64]{0,2,1:T(8,128)(2,1)S(1)}, bf16[1024,16,64]{0,2,1:T(8,128)(2,1)}, u32[]{:S(2)}) copy-start(bf16[1024,16,64]{0,2,1:T(8,128)(2,1)} %get-tuple-element.397) | copy-start | bytes 6291460 | tf_op jit(solution)/shard_map/while
  173.2 15.7 %copy-start.12 = (bf16[2,512,16,64]{1,3,2,0:T(8,128)(2,1)S(1)}, bf16[2,512,16,64]{1,3,2,0:T(8,128)(2,1)}, u32[]{:S(2)}) copy-start(bf16[2,512,16,64]{1,3,2,0:T(8,128)(2,1)} %get-tuple-element.379) | copy-start | bytes 6291460 | tf_op jit(solution)/shard_map/while
  219.5 48.7 %copy-start.46 = (f32[4096]{0:T(1024)S(1)}, f32[4096]{0:T(1024)}, u32[]{:S(2)}) copy-start(f32[4096]{0:T(1024)} %param.28) | copy-start | bytes 49156
  312.3 17.3 %copy-start.15 = (f32[2,16,512]{2,1,0:T(8,128)}, f32[2,16,512]{2,1,0:T(8,128)S(1)}, u32[]{:S(2)}) copy-start(f32[2,16,512]{2,1,0:T(8,128)S(1)} %get-tuple-element.442) | copy-start | bytes 196612 | tf_op jit(solution)/shard_map/while
  413.4 9.8 %copy-start.16 = (f32[2,16,512]{2,1,0:T(8,128)S(1)}, f32[2,16,512]{2,1,0:T(8,128)}, u32[]{:S(2)}) copy-start(f32[2,16,512]{2,1,0:T(8,128)} %copy-done.15) | copy-start | bytes 196612 | tf_op jit(solution)/shard_map/while
  423.2 17.3 %copy-start.15 = (f32[2,16,512]{2,1,0:T(8,128)}, f32[2,16,512]{2,1,0:T(8,128)S(1)}, u32[]{:S(2)}) copy-start(f32[2,16,512]{2,1,0:T(8,128)S(1)} %get-tuple-element.442) | copy-start | bytes 196612 | tf_op jit(solution)/shard_map/while
  526.7 9.8 %copy-start.16 = (f32[2,16,512]{2,1,0:T(8,128)S(1)}, f32[2,16,512]{2,1,0:T(8,128)}, u32[]{:S(2)}) copy-start(f32[2,16,512]{2,1,0:T(8,128)} %copy-done.15) | copy-start | bytes 196612 | tf_op jit(solution)/shard_map/while
  548.0 6.8 copy-start.35
  560.0 17.0 %copy-start.38 = (f32[1024]{0:T(1024)S(1)}, f32[1024]{0:T(1024)}, u32[]{:S(2)}) copy-start(f32[1024]{0:T(1024)} %copy-done.37) | copy-start | bytes 12292
  588.8 87.2 %copy-start.21 = (f32[4,1024,4]{1,2,0:T(4,128)S(1)}, f32[4,1024,4]{1,2,0:T(4,128)}, u32[]{:S(2)}) copy-start(f32[4,1024,4]{1,2,0:T(4,128)} %param.31) | copy-start | bytes 196612
  588.8 87.2 %copy-start.29 = (f32[4,1024,4]{1,2,0:T(4,128)S(1)}, f32[4,1024,4]{1,2,0:T(4,128)}, u32[]{:S(2)}) copy-start(f32[4,1024,4]{1,2,0:T(4,128)} %param.32) | copy-start | bytes 196612
  588.8 88.8 %copy-start.28 = (f32[4,1024,4]{1,2,0:T(4,128)S(1)}, f32[4,1024,4]{1,2,0:T(4,128)}, u32[]{:S(2)}) copy-start(f32[4,1024,4]{1,2,0:T(4,128)} %param.33) | copy-start | bytes 196612
  (37 other events, 120.2 us)
Sparse Core Ops, SparseCore 0:
  10.3 64.5 all-gather.4
  77.0 39.9 all-gather.6
  119.2 73.6 all-gather.8
  195.0 73.1 all-gather.10
  560.1 115.8 all-reduce.1
where the time goes:
time: 696 us; the launch traced here: 686 us
  matrix products  325 us (47%)
  waiting for transfers between devices  168 us (24%)
  other arithmetic  111 us (16%)
  local copies, waits for them, and re-layouts  60.6 us (9%)
  between operations  14.6 us (2%)
  loops' own time  7.13 us (1%)
    psum x1, waiting for transfers between devices, per_device(): adapter_grad = lax.psum(local_grads, ('fsdp', 'dp'))  81.9 us
    dot_general x4, matrix products, block_scores(): jnp.einsum('qhe,khe->hqk', query_block, key_heads, preferred_element_type...  59.7 us
    convert_element_type x2, other arithmetic, one_block(): grad_scores = (probs * (grad_probs - inner)).astype(jnp.bfloat16)  55.6 us
    dot_general x2, matrix products, one_block(): jnp.einsum('qhe,khe->hqk', grad_block, value_heads, preferred_element_typ...  52 us
    all_gather x1, waiting for transfers between devices, per_device(): lax.all_gather(w_qkv, 'fsdp', axis=0, tiled=True)  51.8 us
    dot_general x7, matrix products, contract_trailing(): lax.dot_general(left, right, (((1,), (1,)), ((), ())), preferred_element_...  51.5 us
    dot_general x2, matrix products, one_block(): jnp.einsum('hqk,qhe->khe', probs.astype(jnp.bfloat16), grad_block, prefer...  36.3 us
    all_gather x1, waiting for transfers between devices, per_device(): lax.all_gather(w_proj, 'fsdp', axis=0, tiled=True)  31.9 us
  transfers between devices with their start and end apart: 5, of which 3 were waited for; matrix products, arithmetic and copies ran while one was open for 29% of the time, Pallas kernels for 0%

commit v1 on v0

v1 whole, which is shorter than its diff:
```python
import functools
import jax, jax.numpy as jnp
from jax import lax
from jax.experimental import pallas as pl
from jax.experimental.pallas import tpu as pltpu
from jax.sharding import PartitionSpec as P
F32=jnp.float32; BF=jnp.bfloat16
T=1024; D=1024; H=16; G=4; GW=256
NEG=-1e30
def nn(a,b): return lax.dot_general(a,b,(((1,),(0,)),((),())),preferred_element_type=F32)
def nt(a,b): return lax.dot_general(a,b,(((1,),(1,)),((),())),preferred_element_type=F32)
def tn(a,b): return lax.dot_general(a,b,(((0,),(0,)),((),())),preferred_element_type=F32)
def lane(shape): return lax.broadcasted_iota(jnp.int32,shape,1)
def row(shape): return lax.broadcasted_iota(jnp.int32,shape,0)
def stats(v):
    mu=jnp.mean(v,axis=-1,keepdims=True); c=v-mu
    rs=lax.rsqrt(jnp.mean(c*c,axis=-1,keepdims=True)+1e-5)
    return c,rs
def parts(x):
    hi=x.astype(BF); r1=x-hi.astype(F32); mid=r1.astype(BF); lo=(r1-mid.astype(F32)).astype(BF)
    return hi.astype(F32),mid.astype(F32),lo.astype(F32)
def key_lanes(starts_row):
    l=lane((T,128)); r=row((T,128))
    return jnp.where(l<8, jnp.where(r>=starts_row,0.0,NEG), jnp.where(l<11,-1.0,0.0)).astype(BF)
def query_lanes(cols):
    l=lane((T,128)); r=row((T,128))
    base=jnp.where(l==lax.shift_right_logical(r,7),1.0,0.0)
    if cols is not None:
        hi,mid,lo=cols
        base=jnp.where(l==8,hi,jnp.where(l==9,mid,jnp.where(l==10,lo,base)))
    return base.astype(BF)
QB=256
def attn_fwd_pair(q,k,v,klanes,qlanes):
    l=lane((T,128))
    q8=q*jnp.asarray(0.125,BF)
    ka=jnp.concatenate([k,klanes],axis=1)
    outs=[];lses=[]
    tri=lane((QB,QB))<=row((QB,QB))
    for h in range(2):
        hm=(l<64) if h==0 else (l>=64)
        qa=jnp.concatenate([jnp.where(hm,q8,jnp.zeros_like(q8)),qlanes],axis=1)
        ob=[];lb=[]
        for i in range(T//QB):
            n=(i+1)*QB
            s=nt(qa[i*QB:(i+1)*QB],ka[:n])
            sd=jnp.where(tri,s[:,n-QB:],NEG)
            s=jnp.concatenate([s[:,:n-QB],sd],axis=1) if i else sd
            m=jnp.max(s,axis=1,keepdims=True)
            e=jnp.exp(s-m)
            tot=jnp.sum(e,axis=1,keepdims=True)
            o=nn(e.astype(BF),v[:n])*(1.0/tot)
            ob.append(o); lb.append(m+jnp.log(tot))
        outs.append(ob); lses.append(lb)
    return outs,lses
def fwd_kernel(x_ref,gain_ref,shift_ref,st_ref,w_ref,b_ref,at_ref,uq_ref,uv_ref,q_ref,k_ref,v_ref,o_ref,lse_ref,r_ref,h1_ref,kl_ref,ql_ref):
    g=pl.program_id(0)
    @pl.when(g==0)
    def _():
        def blk(i,_):
            sl=pl.ds(pl.multiple_of(i*256,256),256)
            c,rs=stats(x_ref[sl,:].astype(F32))
            h1_ref[sl,:]=(c*rs*gain_ref[0:1,:]+shift_ref[0:1,:]).astype(BF)
            r_ref[sl,:]=nt(h1_ref[sl,:],at_ref[...]).astype(BF)
            return 0
        lax.fori_loop(0,4,blk,0)
        kl_ref[...]=key_lanes(st_ref[...])
        ql_ref[...]=query_lanes(None)
        lse_ref[...]=jnp.zeros((T,128),F32)
    for i in range(4):
        sl=pl.ds(i*256,256)
        m=nn(h1_ref[sl,:],w_ref[0])+b_ref[0]
        q_ref[sl,:]=(m[:,:256]+nn(r_ref[sl,:],uq_ref[...])).astype(BF)
        k_ref[sl,:]=m[:,256:512].astype(BF)
        v_ref[sl,:]=(m[:,512:]+nn(r_ref[sl,:],uv_ref[...])).astype(BF)
    for p in range(2):
        cs=slice(p*128,p*128+128)
        outs,lses=attn_fwd_pair(q_ref[:,cs],k_ref[:,cs],v_ref[:,cs],kl_ref[...],ql_ref[...])
        lq=lane((QB,128))
        for i in range(T//QB):
            sl=slice(i*QB,(i+1)*QB)
            o_ref[sl,cs]=jnp.where(lq<64,outs[0][i],outs[1][i]).astype(BF)
            hd=g*4+p*2
            lse_ref[sl,:]=jnp.where(lq==hd,lses[0][i],jnp.where(lq==hd+1,lses[1][i],lse_ref[sl,:]))
VM=pl.BlockSpec(memory_space=pltpu.VMEM)
def fwd_call(x,gain,shift,st,w4,b4,at,uq,uv):
    cb=pl.BlockSpec((T,GW),lambda g:(0,g))
    ub=pl.BlockSpec((16,GW),lambda g:(0,g))
    return pl.pallas_call(fwd_kernel,grid=(G,),
      in_specs=[VM,VM,VM,VM,pl.BlockSpec((1,D,3*GW),lambda g:(g,0,0)),pl.BlockSpec((1,1,3*GW),lambda g:(g,0,0)),VM,ub,ub],
      out_specs=[cb,cb,cb,cb,pl.BlockSpec((T,128),lambda g:(0,0)),pl.BlockSpec((T,16),lambda g:(0,0))],
      out_shape=[jax.ShapeDtypeStruct((T,D),BF)]*4+[jax.ShapeDtypeStruct((T,128),F32),jax.ShapeDtypeStruct((T,16),BF)],
      scratch_shapes=[pltpu.VMEM((T,D),BF),pltpu.VMEM((T,128),BF),pltpu.VMEM((T,128),BF)],
      compiler_params=pltpu.CompilerParams(vmem_limit_bytes=58*2**20),name="attend")(x,gain,shift,st,w4,b4,at,uq,uv)

C0=0.7978845608; C1=0.044715
def mid_kernel(x_ref,o_ref,og_ref,gain_ref,shift_ref,ob_ref,wo_ref,wf_ref,bf_ref,wp_ref,bo_ref,dx2_ref,do_ref,x2_ref,h2_ref,dh_ref):
    j=pl.program_id(0); nj=pl.num_programs(0)
    y_ref=dx2_ref
    RB=256
    @pl.when(j==0)
    def _():
        def blk(i,_):
            sl=pl.ds(pl.multiple_of(i*RB,RB),RB)
            x2=x_ref[sl,:].astype(F32)+nn(o_ref[sl,:],wo_ref[...])+ob_ref[0:1,:]
            x2_ref[sl,:]=x2
            c,rs=stats(x2)
            h2_ref[sl,:]=(c*rs*gain_ref[1:2,:]+shift_ref[1:2,:]).astype(BF)
            y_ref[sl,:]=x2+ob_ref[1:2,:]
            dh_ref[sl,:]=jnp.zeros((RB,D),F32)
            return 0
        lax.fori_loop(0,T//RB,blk,0)
    def blk(i,_):
        sl=pl.ds(pl.multiple_of(i*RB,RB),RB)
        f=nn(h2_ref[sl,:],wf_ref[0])+bf_ref[...]
        f2=f*f
        t=jnp.tanh(C0*(f+C1*(f2*f)))
        hp=0.5*(1.0+t)
        g=(f*hp).astype(BF)
        gp=hp+(0.5*C0)*f*(1.0-t*t)*(1.0+(3*C1)*f2)
        y_ref[sl,:]+=nn(g,wp_ref[...])
        dg=nt(og_ref[sl,:],wp_ref[...])
        df=(dg*gp).astype(BF)
        dh_ref[sl,:]+=nt(df,wf_ref[0])
        return 0
    lax.fori_loop(0,T//RB,blk,0)
    @pl.when(j==nj-1)
    def _():
        def blk(i,_):
            sl=pl.ds(pl.multiple_of(i*RB,RB),RB)
            bo_ref[sl,:]=y_ref[sl,:].astype(BF)
            c,rs=stats(x2_ref[sl,:])
            xh=c*rs
            dy=dh_ref[sl,:]*gain_ref[1:2,:]
            dx2=og_ref[sl,:].astype(F32)+rs*(dy-jnp.mean(dy,axis=-1,keepdims=True)-xh*jnp.mean(dy*xh,axis=-1,keepdims=True))
            dx2_ref[sl,:]=dx2
            do_ref[sl,:]=nt(dx2.astype(BF),wo_ref[...]).astype(BF)
            return 0
        lax.fori_loop(0,T//RB,blk,0)
def mid_call(x,o,og,gain,shift,ob,wo,wf4,bfc,wp):
    nf,_,fw=wf4.shape
    return pl.pallas_call(mid_kernel,grid=(nf,),
      in_specs=[VM]*7+[pl.BlockSpec((1,D,fw),lambda j:(j,0,0)),pl.BlockSpec((1,fw),lambda j:(0,j)),pl.BlockSpec((fw,D),lambda j:(j,0))],
      out_specs=[VM,VM,VM],
      out_shape=[jax.ShapeDtypeStruct((T,D),BF),jax.ShapeDtypeStruct((T,D),F32),jax.ShapeDtypeStruct((T,D),BF)],
      scratch_shapes=[pltpu.VMEM((T,D),F32),pltpu.VMEM((T,D),BF),pltpu.VMEM((T,D),F32)],
      compiler_params=pltpu.CompilerParams(vmem_limit_bytes=60*2**20),name="middle")(x,o,og,gain,shift,ob,wo,wf4,bfc,wp)

def attn_bwd_pair(q,k,v,do,o,lcols,klanes,store,KB=256):
    l=lane((T,128))
    q8=q*jnp.asarray(0.125,BF)
    ka=jnp.concatenate([k,klanes],axis=1)
    vl=jnp.where((l>=8)&(l<11),-1.0,0.0).astype(BF)
    va=jnp.concatenate([v,vl],axis=1)
    prod=do.astype(F32)*o.astype(F32)
    causal=row((KB,KB))<=lane((KB,KB))
    res=[]
    for h in range(2):
        hm=(l<64) if h==0 else (l>=64)
        dcol=jnp.sum(jnp.where(hm,prod,0.0),axis=1,keepdims=True)
        qa=jnp.concatenate([jnp.where(hm,q8,jnp.zeros_like(q8)),query_lanes(parts(lcols[h]))],axis=1)
        hi,mid,lo=parts(dcol)
        dl=jnp.where(l==8,hi,jnp.where(l==9,mid,jnp.where(l==10,lo,0.0))).astype(BF)
        da=jnp.concatenate([jnp.where(hm,do,jnp.zeros_like(do)),dl],axis=1)
        dqs=[None]*(T//KB); dks=[];dvs=[]
        for j in range(T//KB):
            r0=j*KB
            t=nt(ka[r0:r0+KB],qa[r0:])
            td=jnp.where(causal,t[:,:KB],NEG)
            t=jnp.concatenate([td,t[:,KB:]],axis=1) if r0+KB<T else td
            p=jnp.exp(t)
            dvs.append(nn(p.astype(BF),do[r0:]))
            u=nt(va[r0:r0+KB],da[r0:])
            ds=(p*u).astype(BF)
            dks.append(nn(ds,q8[r0:]))
            dq=tn(ds,k[r0:r0+KB])
            for i in range(j,T//KB):
                piece=dq[(i-j)*KB:(i-j+1)*KB]
                dqs[i]=piece if dqs[i] is None else dqs[i]+piece
        res.append((dqs,dks,dvs))
    lk=lane((KB,128))<64
    for i in range(T//KB):
        sl=slice(i*KB,(i+1)*KB)
        store("q",sl,jnp.where(lk,res[0][0][i],res[1][0][i])*0.125)
        store("k",sl,jnp.where(lk,res[0][1][i],res[1][1][i]))
        store("v",sl,jnp.where(lk,res[0][2][i],res[1][2][i]))
def bwd_kernel(x_ref,gain_ref,shift_ref,st_ref,w_ref,at_ref,uq_ref,uv_ref,r_ref,lse_ref,q_ref,k_ref,v_ref,do_ref,o_ref,dx2_ref,ig_ref,ga_ref,kl_ref,dm_ref,dh_ref,dr_ref,gs_ref):
    g=pl.program_id(0)
    @pl.when(g==0)
    def _():
        kl_ref[...]=key_lanes(st_ref[...])
        dr_ref[...]=jnp.zeros((T,16),F32)
    l=lane((T,128))
    for p in range(2):
        cs=slice(p*128,p*128+128)
        hd=g*4+p*2
        lse=lse_ref[...]
        lc=[jnp.sum(jnp.where(l==hd+h,lse,0.0),axis=1,keepdims=True) for h in range(2)]
        def store(kind,sl,val):
            off={"q":0,"k":256,"v":512}[kind]+p*128
            dm_ref[sl,off:off+128]=val.astype(BF)
        attn_bwd_pair(q_ref[:,cs],k_ref[:,cs],v_ref[:,cs],do_ref[:,cs],o_ref[:,cs],lc,kl_ref[...],store)
    dq=dm_ref[:,:256]; dv=dm_ref[:,512:]
    dr_ref[...]+=nt(dq,uq_ref[...])+nt(dv,uv_ref[...])
    ra=row((16,256))
    gu=8.0*(jnp.where((ra>=4)&(ra<8),tn(r_ref[...],dq),0.0)+jnp.where(ra>=12,tn(r_ref[...],dv),0.0))
    gs_ref[:,pl.ds(pl.multiple_of(g*256,256),256)]=gu
    @pl.when(g==0)
    def _():
        for i in range(4):
            sl=slice(i*256,(i+1)*256)
            dh_ref[sl,:]=nt(dm_ref[sl,:],w_ref[0])
    @pl.when(g>0)
    def _():
        for i in range(4):
            sl=slice(i*256,(i+1)*256)
            dh_ref[sl,:]+=nt(dm_ref[sl,:],w_ref[0])
    @pl.when(g==G-1)
    def _():
        def blk(i,_):
            sl=pl.ds(pl.multiple_of(i*256,256),256)
            drb=dr_ref[sl,:].astype(BF)
            dh=dh_ref[sl,:]+nn(drb,at_ref[...])
            c,rs=stats(x_ref[sl,:].astype(F32))
            xh=c*rs
            h1=(xh*gain_ref[0:1,:]+shift_ref[0:1,:]).astype(BF)
            dy=dh*gain_ref[0:1,:]
            ig_ref[sl,:]=dx2_ref[sl,:]+rs*(dy-jnp.mean(dy,axis=-1,keepdims=True)-xh*jnp.mean(dy*xh,axis=-1,keepdims=True))
            gs_ref[...]+=tn(drb,h1)
            return 0
        lax.fori_loop(0,4,blk,0)
        for i in range(4):
            ga_ref[i]=gs_ref[4*i:4*i+4,:]
def bwd_call(x,gain,shift,st,w4,at,uq,uv,r,lse,q,k,v,do,o,dx2):
    cb=pl.BlockSpec((T,GW),lambda g:(0,g))
    ub=pl.BlockSpec((16,GW),lambda g:(0,g))
    return pl.pallas_call(bwd_kernel,grid=(G,),
      in_specs=[VM,VM,VM,VM,pl.BlockSpec((1,D,3*GW),lambda g:(g,0,0)),VM,ub,ub,VM,VM,cb,cb,cb,cb,cb,VM],
      out_specs=[VM,VM],
      out_shape=[jax.ShapeDtypeStruct((T,D),F32),jax.ShapeDtypeStruct((4,4,D),F32)],
      scratch_shapes=[pltpu.VMEM((T,128),BF),pltpu.VMEM((T,768),BF),pltpu.VMEM((T,D),F32),pltpu.VMEM((T,16),F32),pltpu.VMEM((16,D),F32)],
      compiler_params=pltpu.CompilerParams(vmem_limit_bytes=60*2**20),name="back")(x,gain,shift,st,w4,at,uq,uv,r,lse,q,k,v,do,o,dx2)
MESH=pl.DeviceIdType.MESH

def make_gather(A,B,chunks,offs=(0,2,3,5,6)):
    L1a = A>=B
    L1,L2 = (A,B) if L1a else (B,A)
    n=len(chunks)
    def setup():
        f = lax.axis_index("fsdp"); d = lax.axis_index("dp")
        c = lax.rem(f,2); h=lax.div(f,2); b = lax.rem(h,B); a = lax.div(h,B)
        par=lax.rem(d,2); xp = d+1-2*par
        return f,d,a,b,c,par,xp
    def dev(a_,b_,c_,d_):
        return {"fsdp": (a_*B+b_)*2+c_, "dp": d_}
    def run(w_refs,o_refs,S, tick=None):
        f,d,a,b,c,par,xp=setup()
        if L1a:
            l1=lambda k: (lax.rem(a+k,A),b); l2=lambda k:(a,lax.rem(b+k,B));
            l1m=lambda k: (lax.rem(a+A-k,A),b)
        else:
            l1=lambda k: (a,lax.rem(b+k,B)); l2=lambda k:(lax.rem(a+k,A),b)
            l1m=lambda k: (a,lax.rem(b+B-k,B))
        bar=pltpu.get_barrier_semaphore()
        peers=[dev(a,b,1-c,d),dev(a,b,c,xp)]+[dev(*l1(k),c,d) for k in range(1,L1)]+[dev(*l2(k),c,d) for k in range(1,L2)]
        for p in peers: pl.semaphore_signal(bar,inc=1,device_id=p,device_id_type=MESH)
        def view(g,aa,bb,cc,cols):
            ch=chunks[g]; o=o_refs[ch["out"]]
            idx=(ch["osel"],) if ch["osel"] is not None else ()
            return o.at[idx+(aa,bb,cc,pl.ds(ch["r0"],ch["rows"]),cols)]
        def width(g): return sum(w for _,w in chunks[g]["cols"])
        def carried(g):
            ch=chunks[g]; N=width(g); xc=ch["xc"]
            return pl.ds(pl.multiple_of(par*xc,128),N-xc)
        def xsend(g):
            ch=chunks[g]; N=width(g); xc=ch["xc"]
            return pl.ds(pl.multiple_of(par*(N-xc),128),xc)
        def xrecv(g):
            ch=chunks[g]; N=width(g); xc=ch["xc"]
            return pl.ds(pl.multiple_of((1-par)*(N-xc),128),xc)
        loc=[]
        for g in range(n):
            ch=chunks[g]; w=w_refs[ch["src"]]; off=0; lst=[]
            for i,(c0,wd) in enumerate(ch["cols"]):
                cp=pltpu.make_async_copy(w.at[pl.ds(ch["r0"],ch["rows"]),pl.ds(c0,wd)], view(g,a,b,c,pl.ds(off,wd)), S["loc"].at[g,i])
                cp.start(); lst.append(cp); off+=wd
            loc.append(lst)
        pl.semaphore_wait(bar,len(peers))
        def rc(src,dst,ss,rs,to):
            return pltpu.make_async_remote_copy(src_ref=src,dst_ref=dst,send_sem=ss,recv_sem=rs,device_id=to,device_id_type=MESH)
        pend=[]
        st={}
        def stage0(g):
            for cp in loc[g]: cp.wait()
            v=view(g,a,b,c,carried(g)); cps=[]
            for k in range(1,L1):
                cp=rc(v,v,S["zs"].at[g,k-1],S["zr"].at[g,k-1],dev(*l1(k),c,d)); cp.start(); cps.append(cp)
            st[g]=cps; pend.extend(cps)
        def stage1(g):
            for k,cp in enumerate(st[g]):
                cp.wait_recv()
            sl=carried(g)
            v = view(g,slice(None),b,c,sl) if L1a else view(g,a,slice(None),c,sl)
            cps=[]
            for k in range(1,L2):
                cp=rc(v,v,S["ys"].at[g,k-1],S["yr"].at[g,k-1],dev(*l2(k),c,d)); cp.start(); cps.append(cp)
            xs=[]
            for k in range(1,L1):
                aa,bb=l1(k); v=view(g,aa,bb,c,xsend(g))
                cp=rc(v,v,S["x1s"].at[g,k-1],S["x1r"].at[g,k-1],dev(a,b,c,xp)); cp.start(); xs.append(cp)
            st[g]=(cps,xs); pend.extend(cps); pend.extend(xs)
        def stage2(g):
            cps,xs=st[g]; ys=[]
            for k,cp in enumerate(cps,1):
                cp.wait_recv()
            for k,cp in enumerate(cps,1):
                aa,bb=l2(k)
                v = view(g,slice(None),bb,c,xsend(g)) if L1a else view(g,aa,slice(None),c,xsend(g))
                x=rc(v,v,S["x2s"].at[g,k-1],S["x2r"].at[g,k-1],dev(a,b,c,xp)); x.start(); ys.append(x)
            st[g]=(xs,ys); pend.extend(ys)
        def stage3(g):
            xs,ys=st[g]
            for cp in xs+ys: cp.wait_recv()
            v=view(g,slice(None),slice(None),c,pl.ds(0,width(g)))
            cp=rc(v,v,S["cs"].at[g],S["cr"].at[g],dev(a,b,1-c,d)); cp.start(); st[g]=cp; pend.append(cp)
        def stage4(g):
            st[g].wait_recv()
        stages=[stage0,stage1,stage2,stage3,stage4]
        for t in range(n+offs[-1]):
            for s in range(len(stages)):
                g=t-offs[s]
                if 0<=g<n: stages[s](g)
            if tick is not None: tick(t)
        for cp in pend: cp.wait_send()
    sems=dict(loc=(n,max(len(ch["cols"]) for ch in chunks)),zs=(n,L1-1),zr=(n,L1-1),ys=(n,L2-1),yr=(n,L2-1),x1s=(n,L1-1),x1r=(n,L1-1),x2s=(n,L2-1),x2r=(n,L2-1),cs=(n,),cr=(n,))
    return run,sems

def gather_chunks(R,RP,nf=4,qs=2,rs=2):
    ch=[]
    for j in range(G):
        for r in range(qs):
            ch.append(dict(src=0,out=0,osel=j,r0=R//qs*r,rows=R//qs,cols=[(D*p+GW*j,GW) for p in range(3)],xc=GW))
    for r in range(rs):
        ch.append(dict(src=1,out=1,osel=None,r0=R//rs*r,rows=R//rs,cols=[(0,D)],xc=384))
    w_=4*D//nf; r_=RP//nf
    for j in range(nf):
        for r in range(rs):
            ch.append(dict(src=2,out=2,osel=j,r0=R//rs*r,rows=R//rs,cols=[(w_*j,w_)],xc=384))
        for r in range(rs):
            ch.append(dict(src=3,out=3,osel=None,r0=r_*j+r_//rs*r,rows=r_//rs,cols=[(0,D)],xc=384))
    return ch
def gather_call(A,B,wq,wo,wf,wp):
    R=wq.shape[0]; RP=wp.shape[0]
    run,sems=make_gather(A,B,gather_chunks(R,RP),(0,2,3,4,5))
    names=list(sems)
    def body(*refs):
        run(refs[:4],refs[4:8],dict(zip(names,refs[8:])))
    outs=[(G,A,B,2,R,3*GW),(A,B,2,R,D),(4,A,B,2,R,D),(A,B,2,RP,D)]
    hbm=pl.BlockSpec(memory_space=pl.ANY)
    o=pl.pallas_call(body,in_specs=[VM]*4,out_specs=[hbm]*4,out_shape=[jax.ShapeDtypeStruct(s,BF) for s in outs],
      scratch_shapes=[pltpu.SemaphoreType.DMA(s) for s in sems.values()],
      compiler_params=pltpu.CompilerParams(collective_id=0,has_side_effects=True,vmem_limit_bytes=16*2**20),name="gather")(wq,wo,wf,wp)
    return o[0].reshape(G,D,3*GW),o[1].reshape(D,D),o[2].reshape(4,D,D),o[3].reshape(4*D,D)

def sum_kernel(F,DP,g_ref,o_ref,acc_ref,rcv_ref,ss,rs):
    f=lax.axis_index("fsdp"); d=lax.axis_index("dp")
    partners=[]
    for ax,size,me in (("fsdp",F,f),("dp",DP,d)):
        bit=1
        while bit<size:
            other=me+bit-2*bit*lax.rem(lax.div(me,bit),2)
            partners.append({"fsdp":other,"dp":d} if ax=="fsdp" else {"fsdp":f,"dp":other})
            bit*=2
    bar=pltpu.get_barrier_semaphore()
    for p in partners: pl.semaphore_signal(bar,inc=1,device_id=p,device_id_type=MESH)
    pl.semaphore_wait(bar,len(partners))
    acc_ref[0]=g_ref[...]
    cps=[]
    for s,p in enumerate(partners):
        cp=pltpu.make_async_remote_copy(src_ref=acc_ref.at[s],dst_ref=rcv_ref.at[s],send_sem=ss.at[s],recv_sem=rs.at[s],device_id=p,device_id_type=MESH)
        cp.start(); cps.append(cp)
        cp.wait_recv()
        tot=acc_ref[s]+rcv_ref[s]
        if s+1<len(partners): acc_ref[s+1]=tot
        else: o_ref[...]=tot
    for cp in cps: cp.wait_send()
def sum_call(F,DP,g):
    n=(F.bit_length()-1)+(DP.bit_length()-1)
    return pl.pallas_call(functools.partial(sum_kernel,F,DP),in_specs=[VM],out_specs=VM,out_shape=jax.ShapeDtypeStruct(g.shape,F32),
      scratch_shapes=[pltpu.VMEM((n,)+g.shape,F32),pltpu.VMEM((n,)+g.shape,F32),pltpu.SemaphoreType.DMA((n,)),pltpu.SemaphoreType.DMA((n,))],
      compiler_params=pltpu.CompilerParams(collective_id=1,has_side_effects=True),name="total")(g)

def adapters_prep(ad):
    a=ad.astype(BF).transpose(0,2,1)
    at=jnp.concatenate([a[0],a[0],a[2],a[2]],0)
    z=jnp.zeros((4,D),BF); u8=a*jnp.asarray(8,BF)
    uq=jnp.concatenate([u8[1],z,z,z],0); uv=jnp.concatenate([z,z,u8[3],z],0)
    return at,uq,uv
def solution(mesh):
    F=mesh.shape["fsdp"]; DP=mesh.shape["dp"]
    A,B=(F//4,2) if F<=16 else (2,F//4)
    def per_device(tokens,item_start,og,gains,shifts,wqkv,bqkv,wout,wfc,bfc,wproj,ob,adapters,momentum,average):
        b4=bqkv.reshape(3,4,256).transpose(1,0,2).reshape(4,1,768)
        at,uq,uv=adapters_prep(adapters)
        st=jnp.pad(item_start[::128],(0,120)).reshape(1,128)
        w4,wo,wf4,wp=gather_call(A,B,wqkv,wout,wfc,wproj)
        q,k,v,o,lse,r=fwd_call(tokens,gains,shifts,st,w4,b4,at,uq,uv)
        bo,dx2,do=mid_call(tokens,o,og,gains,shifts,ob,wo,wf4,bfc.reshape(1,-1),wp)
        ig,ga=bwd_call(tokens,gains,shifts,st,w4,at,uq,uv,r,lse,q,k,v,do,o,dx2)
        grad=sum_call(F,DP,ga).transpose(0,2,1)
        rate=0.01/jnp.sqrt(jnp.float32(tokens.shape[0]*F*DP))
        mom=0.9*momentum+grad
        new=adapters-rate*(grad+0.9*mom)
        avg=0.9*average+0.1*new
        return bo,ig,grad,mom,new,avg,new.astype(BF)
    rows=P(("fsdp","dp"),None); w=P("fsdp",None); n=P()
    return jax.shard_map(per_device,mesh=mesh,
      in_specs=(rows,P(("fsdp","dp")),rows,n,n,w,n,w,w,n,w,n,n,n,n),out_specs=(rows,rows,n,n,n,n,n),check_vma=False)
```

time: 696 us -> 310 us (0.45); the launches traced: 686 us -> 309 us
  matrix products: 325 us -> 0 us
  Pallas kernels: 0 us -> 285 us
  waiting for transfers between devices: 168 us -> 0 us
  other arithmetic: 111 us -> 4.37 us
  local copies, waits for them, and re-layouts: 60.6 us -> 19.3 us
  between operations: 14.6 us -> 0.72 us
  loops' own time: 7.13 us -> 0 us
    dot_general x33 -> x0, matrix products: 325 us -> none  [the longest x4 59.7 us: block_scores(): jnp.einsum('qhe,khe->hqk', query_block, key_heads, preferred_element_type...]
    pallas_call x0 -> x5, Pallas kernels: none -> 285 us  [the longest x1 112 us: gather_call(): pl.pallas_call(body, in_specs=[VM] * 4, out_specs=[hbm] * 4, out_shape=[j...]
    all_gather x4 -> x0, waiting for transfers between devices: 83.7 us -> none  [the longest x1 51.8 us: per_device(): lax.all_gather(w_qkv, 'fsdp', axis=0, tiled=True)]
    psum x1 -> x0, waiting for transfers between devices: 81.9 us -> none  [per_device(): adapter_grad = lax.psum(local_grads, ('fsdp', 'dp'))]
    convert_element_type x7 -> x1, other arithmetic: 60.9 us -> 1.53 us  [per_device(): return (bo, ig, grad, mom, new, avg, new.astype(BF))]
    reduce_sum x7 -> x0, other arithmetic: 38.6 us -> none  [the longest x2 31.5 us: one_block(): totals = jnp.sum(raised, axis=-1, keepdims=True)]
    unnamed x99 -> x25, local copies, waits for them, and re-layouts: 30.4 us -> 15.9 us
    while x22 -> x0, local copies, waits for them, and re-layouts: 8.55 us -> none  [the longest x1 3.76 us: attend_forward(): lax.map(one_block, jnp.arange(row_count // span_rows, dtype=jnp.int32))]
  transfers between devices with their start and end apart: 5 -> 0, of which waited for: 3 -> 0; matrix products, arithmetic and copies ran while one was open for 29% -> 0% of each run, Pallas kernels for 0% -> 0%
where the time goes in v1:
time: 310 us; the launch traced here: 309 us
  Pallas kernels  285 us (92%)
  local copies, waits for them, and re-layouts  19.3 us (6%)
  other arithmetic  4.37 us (1%)
    pallas_call x1, Pallas kernels, gather_call(): pl.pallas_call(body, in_specs=[VM] * 4, out_specs=[hbm] * 4, out_shape=[j...  112 us
    pallas_call x1, Pallas kernels, mid_call(): pl.pallas_call(mid_kernel, grid=(nf,), in_specs=[VM] * 7 + [pl.BlockSpec(...  56.9 us
    pallas_call x1, Pallas kernels, bwd_call(): pl.pallas_call(bwd_kernel, grid=(G,), in_specs=[VM, VM, VM, VM, pl.BlockS...  55.9 us
    pallas_call x1, Pallas kernels, fwd_call(): pl.pallas_call(fwd_kernel, grid=(G,), in_specs=[VM, VM, VM, VM, pl.BlockS...  39.7 us
    pallas_call x1, Pallas kernels, sum_call(): pl.pallas_call(functools.partial(sum_kernel, F, DP), in_specs=[VM], out_s...  20.6 us
    unnamed x25, local copies, waits for them, and re-layouts  15.9 us

profile of v1, /device:TPU:0, one launch (start us, length us, event | category | flops | bytes accessed | tf_op | source)
XLA Modules:
  0.0 309.1 jit_solution(15103050077808030272)
XLA Ops:
  0.6 0.8 slice.17
  1.4 0.5 pad_bitcast_fusion.st_ref
  2.0 0.7 reshape.40
  2.7 0.6 copy.22.b_ref
  3.3 0.9 broadcast_multiply_fusion
  4.2 0.7 maximum_maximum_fusion.uv_ref
  4.9 0.6 concatenate.14.uq_ref
  5.5 0.6 pad_maximum_fusion.at_ref
  6.2 1.0 copy-done.4
  7.2 1.0 copy-done.5
  8.3 1.0 copy-done.6
  9.3 0.9 copy-done.7
  10.2 111.7 %gather.1 = (bf16[4,4,2,2,64,768]{5,4,3,2,1,0:T(8,128)(2,1)S(1)}, bf16[4,2,2,64,1024]{4,3,2,1,0:T(8,128)(2,1)S(1)}, bf16[4,4,2,2,64,1024]{5,4,3,2,1,0:T(8,128)(2,1)S(1)}, bf16[4,2,2,256,1024]{4,3,2,1,0:T(8,128)(2,1)S(1)}) custom-call(bf16[64,3072]{1,0:T(8,128)(2,1)S(1)} %copy-done.6, bf16[64,1024]{1,0:T(8,128)(2,1)S(1)} %copy-done.7, ...), custom_call_target="tpu_custom_call" | custom-call | tf_op jit(solution)/shard_map/gather/pallas_call | solution.py:359
  121.8 2.6 copy-done
  124.5 3.2 %copy-done.1 = bf16[4,4,2,2,64,1024]{5,4,3,2,1,0:T(8,128)(2,1)} copy-done((bf16[4,4,2,2,64,1024]{5,4,3,2,1,0:T(8,128)(2,1)}, bf16[4,4,2,2,64,1024]{5,4,3,2,1,0:T(8,128)(2,1)S(1)}, u32[]{:S(2)}) %copy-start.1) | copy-done | bytes 8388632
  127.7 3.2 %copy-done.2 = bf16[4,2,2,256,1024]{4,3,2,1,0:T(8,128)(2,1)} copy-done((bf16[4,2,2,256,1024]{4,3,2,1,0:T(8,128)(2,1)}, bf16[4,2,2,256,1024]{4,3,2,1,0:T(8,128)(2,1)S(1)}, u32[]{:S(2)}) %copy-start.2) | copy-done | bytes 8388632
  131.0 1.3 copy-done.3
  132.3 39.7 %attend.1 = (bf16[1024,1024]{1,0:T(8,128)(2,1)}, bf16[1024,1024]{1,0:T(8,128)(2,1)}, bf16[1024,1024]{1,0:T(8,128)(2,1)}, bf16[1024,1024]{1,0:T(8,128)(2,1)}, f32...) custom-call(bf16[1024,1024]{1,0:T(8,128)(2,1)} %x_ref.5, f32[2,1024]{1,0:T(2,128)} %gain_ref.5, f32[2,1024]{1,0:T(2,128)} %shift_ref.5, ...), custom_call_target="tpu_custom_call" | custom-call | tf_op jit(solution)/shard_map/attend/pallas_call | solution.py:88
  172.0 56.9 %middle.1 = (bf16[1024,1024]{1,0:T(8,128)(2,1)}, f32[1024,1024]{1,0:T(8,128)}, bf16[1024,1024]{1,0:T(8,128)(2,1)}) custom-call(bf16[1024,1024]{1,0:T(8,128)(2,1)} %x_ref.5, bf16[1024,1024]{1,0:T(8,128)(2,1)} %get-tuple-element.23.o_ref, bf16[1024,1024]{1,0:T(8,128)(2,1)} %og_ref.1, f32[2,1024]{1,0:T(2,128)} %gain_ref.5, f32[2,1024]{1,0:T(2,128)} %shift_ref.5, ...), custom_call_target="tpu_custom_call" | custom-call | tf_op jit(solution)/shard_map/middle/pallas_call | solution.py:141
  228.9 55.9 %back.1 = (f32[1024,1024]{1,0:T(8,128)}, f32[4,4,1024]{2,1,0:T(4,128)}) custom-call(bf16[1024,1024]{1,0:T(8,128)(2,1)} %x_ref.5, f32[2,1024]{1,0:T(2,128)} %gain_ref.5, f32[2,1024]{1,0:T(2,128)} %shift_ref.5, s32[1,128]{1,0:T(1,128)} %pad_bitcast_fusion.st_ref, bf16[4,1024,768]{2,1,0:T(8,128)(2,1)} %bitcast.24, bf16[16,1024]{1,0:T(8,128)(2,1)} %pad_maximum_fusion.at_ref, ...), custom_call_target="tpu_custom_call" | custom-call | tf_op jit(solution)/shard_map/back/pallas_call | solution.py:236
  284.9 20.6 %total.1 = f32[4,4,1024]{2,1,0:T(4,128)} custom-call(f32[4,4,1024]{2,1,0:T(4,128)} %get-tuple-element.36.g_ref), custom_call_target="tpu_custom_call" | custom-call | tf_op jit(solution)/shard_map/total/pallas_call | solution.py:388
  305.5 1.5 fusion
  307.0 0.7 multiply_add_fusion
  307.6 1.5 copy.24
  (21 shorter events, 0.1 us)
Async XLA Ops:
  6.2 1.0 copy-start.4
  7.2 1.0 copy-start.5
  8.3 1.0 copy-start.6
  9.3 0.9 copy-start.7
  121.8 2.7 copy-start
  124.5 3.2 %copy-start.1 = (bf16[4,4,2,2,64,1024]{5,4,3,2,1,0:T(8,128)(2,1)}, bf16[4,4,2,2,64,1024]{5,4,3,2,1,0:T(8,128)(2,1)S(1)}, u32[]{:S(2)}) copy-start(bf16[4,4,2,2,64,1024]{5,4,3,2,1,0:T(8,128)(2,1)S(1)} %get-tuple-element.25) | copy-start | bytes 25165828
  127.7 3.2 %copy-start.2 = (bf16[4,2,2,256,1024]{4,3,2,1,0:T(8,128)(2,1)}, bf16[4,2,2,256,1024]{4,3,2,1,0:T(8,128)(2,1)S(1)}, u32[]{:S(2)}) copy-start(bf16[4,2,2,256,1024]{4,3,2,1,0:T(8,128)(2,1)S(1)} %get-tuple-element.26) | copy-start | bytes 25165828
  131.0 1.3 copy-start.3
  228.9 76.5 %copy-start.9 = (f32[4,1024,4]{1,2,0:T(4,128)S(1)}, f32[4,1024,4]{1,2,0:T(4,128)}, u32[]{:S(2)}) copy-start(f32[4,1024,4]{1,2,0:T(4,128)} %param.27) | copy-start | bytes 196612
  228.9 76.5 %copy-start.11 = (f32[4,1024,4]{1,2,0:T(4,128)S(1)}, f32[4,1024,4]{1,2,0:T(4,128)}, u32[]{:S(2)}) copy-start(f32[4,1024,4]{1,2,0:T(4,128)} %param.28) | copy-start | bytes 196612
  228.9 78.1 %copy-start.10 = (f32[4,1024,4]{1,2,0:T(4,128)S(1)}, f32[4,1024,4]{1,2,0:T(4,128)}, u32[]{:S(2)}) copy-start(f32[4,1024,4]{1,2,0:T(4,128)} %param.29) | copy-start | bytes 196612
  307.0 2.1 copy-start.8

commit v2 on v1

v2 whole, which is shorter than its diff:
```python
import functools
import jax, jax.numpy as jnp
from jax import lax
from jax.experimental import pallas as pl
from jax.experimental.pallas import tpu as pltpu
from jax.sharding import PartitionSpec as P
F32=jnp.float32; BF=jnp.bfloat16
T=1024; D=1024; H=16; G=4; GW=256
NEG=-1e30
def nn(a,b): return lax.dot_general(a,b,(((1,),(0,)),((),())),preferred_element_type=F32)
def nt(a,b): return lax.dot_general(a,b,(((1,),(1,)),((),())),preferred_element_type=F32)
def tn(a,b): return lax.dot_general(a,b,(((0,),(0,)),((),())),preferred_element_type=F32)
def lane(shape): return lax.broadcasted_iota(jnp.int32,shape,1)
def row(shape): return lax.broadcasted_iota(jnp.int32,shape,0)
def stats(v):
    mu=jnp.mean(v,axis=-1,keepdims=True); c=v-mu
    rs=lax.rsqrt(jnp.mean(c*c,axis=-1,keepdims=True)+1e-5)
    return c,rs
def parts(x):
    hi=x.astype(BF); r1=x-hi.astype(F32); mid=r1.astype(BF); lo=(r1-mid.astype(F32)).astype(BF)
    return hi.astype(F32),mid.astype(F32),lo.astype(F32)
def key_lanes(starts_row):
    l=lane((T,128)); r=row((T,128))
    return jnp.where(l<8, jnp.where(r>=starts_row,0.0,NEG), jnp.where(l<11,-1.0,0.0)).astype(BF)
def query_lanes(cols):
    l=lane((T,128)); r=row((T,128))
    base=jnp.where(l==lax.shift_right_logical(r,7),1.0,0.0)
    if cols is not None:
        hi,mid,lo=cols
        base=jnp.where(l==8,hi,jnp.where(l==9,mid,jnp.where(l==10,lo,base)))
    return base.astype(BF)
QB=256
VM=pl.BlockSpec(memory_space=pltpu.VMEM)
C0=0.7978845608; C1=0.044715
def attn_bwd_pair(q,k,v,do,o,lcols,klanes,store,KB=256):
    l=lane((T,128))
    q8=q*jnp.asarray(0.125,BF)
    ka=jnp.concatenate([k,klanes],axis=1)
    vl=jnp.where((l>=8)&(l<11),-1.0,0.0).astype(BF)
    va=jnp.concatenate([v,vl],axis=1)
    prod=do.astype(F32)*o.astype(F32)
    causal=row((KB,KB))<=lane((KB,KB))
    res=[]
    for h in range(2):
        hm=(l<64) if h==0 else (l>=64)
        dcol=jnp.sum(jnp.where(hm,prod,0.0),axis=1,keepdims=True)
        qa=jnp.concatenate([jnp.where(hm,q8,jnp.zeros_like(q8)),query_lanes(parts(lcols[h]))],axis=1)
        hi,mid,lo=parts(dcol)
        dl=jnp.where(l==8,hi,jnp.where(l==9,mid,jnp.where(l==10,lo,0.0))).astype(BF)
        da=jnp.concatenate([jnp.where(hm,do,jnp.zeros_like(do)),dl],axis=1)
        dqs=[None]*(T//KB); dks=[];dvs=[]
        for j in range(T//KB):
            r0=j*KB
            t=nt(ka[r0:r0+KB],qa[r0:])
            td=jnp.where(causal,t[:,:KB],NEG)
            t=jnp.concatenate([td,t[:,KB:]],axis=1) if r0+KB<T else td
            p=jnp.exp(t)
            dvs.append(nn(p.astype(BF),do[r0:]))
            u=nt(va[r0:r0+KB],da[r0:])
            ds=(p*u).astype(BF)
            dks.append(nn(ds,q8[r0:]))
            dq=tn(ds,k[r0:r0+KB])
            for i in range(j,T//KB):
                piece=dq[(i-j)*KB:(i-j+1)*KB]
                dqs[i]=piece if dqs[i] is None else dqs[i]+piece
        res.append((dqs,dks,dvs))
    lk=lane((KB,128))<64
    for i in range(T//KB):
        sl=slice(i*KB,(i+1)*KB)
        store("q",sl,jnp.where(lk,res[0][0][i],res[1][0][i])*0.125)
        store("k",sl,jnp.where(lk,res[0][1][i],res[1][1][i]))
        store("v",sl,jnp.where(lk,res[0][2][i],res[1][2][i]))
MESH=pl.DeviceIdType.MESH

NU=12; NC=24; OFFS=(0,2,3,4,5); NT=NC+OFFS[-1]
class Gather:
    def __init__(self,A,B,l_ref,u_ref,S):
        self.A,self.B,self.l,self.u,self.S=A,B,l_ref,u_ref,S
        self.hr=u_ref.shape[4]//2
        f=lax.axis_index("fsdp"); d=lax.axis_index("dp")
        self.d=d; self.c=lax.rem(f,2); h=lax.div(f,2); self.b=lax.rem(h,B); self.a=lax.div(h,B)
        self.par=lax.rem(d,2); self.xp=d+1-2*self.par
        self.long_a=A>=B; self.L1,self.L2=(A,B) if A>=B else (B,A)
        self.xc=384
    def dev(self,a,b,c,d): return {"fsdp":(a*self.B+b)*2+c,"dp":d}
    def along_a(self,k): return lax.rem(self.a+k,self.A),self.b
    def along_b(self,k): return self.a,lax.rem(self.b+k,self.B)
    def l1(self,k): return self.along_a(k) if self.long_a else self.along_b(k)
    def l2(self,k): return self.along_b(k) if self.long_a else self.along_a(k)
    def peers(self):
        me=(self.a,self.b)
        return [self.dev(*me,1-self.c,self.d),self.dev(*me,self.c,self.xp)]+[self.dev(*self.l1(k),self.c,self.d) for k in range(1,self.L1)]+[self.dev(*self.l2(k),self.c,self.d) for k in range(1,self.L2)]
    def greet(self):
        self.bar=pltpu.get_barrier_semaphore()
        for p in self.peers(): pl.semaphore_signal(self.bar,inc=1,device_id=p,device_id_type=MESH)
    def greeted(self): pl.semaphore_wait(self.bar,len(self.peers()))
    def rows(self,g): return lax.div(g,2),pl.ds(pl.multiple_of(lax.rem(g,2)*self.hr,8),self.hr)
    def view(self,g,a,b,c,cols):
        u,r=self.rows(g)
        return self.u.at[u,a,b,c,r,cols]
    def carried(self): return pl.ds(pl.multiple_of(self.par*self.xc,128),D-self.xc)
    def crossed(self): return pl.ds(pl.multiple_of(self.par*(D-self.xc),128),self.xc)
    def own(self,g):
        u,r=self.rows(g)
        return pltpu.make_async_copy(self.l.at[u,r],self.view(g,self.a,self.b,self.c,slice(None)),self.S["loc"].at[g])
    def rc(self,src,dst,name,idx,to):
        return pltpu.make_async_remote_copy(src_ref=src,dst_ref=dst,send_sem=self.S[name+"s"].at[idx],recv_sem=self.S[name+"r"].at[idx],device_id=to,device_id_type=MESH)
    def zs(self,g):
        u,r=self.rows(g); s=self.l.at[u,r,self.carried()]; t=self.view(g,self.a,self.b,self.c,self.carried())
        return [self.rc(s,t,"z",(g,k-1),self.dev(*self.l1(k),self.c,self.d)) for k in range(1,self.L1)]
    def line(self,g,k,cols):
        a,b=self.l2(k) if k else (self.a,self.b)
        return self.view(g,slice(None),b,self.c,cols) if self.long_a else self.view(g,a,slice(None),self.c,cols)
    def ys(self,g):
        v=self.line(g,0,self.carried())
        return [self.rc(v,v,"y",(g,k-1),self.dev(*self.l2(k),self.c,self.d)) for k in range(1,self.L2)]
    def xs(self,g):
        to=self.dev(self.a,self.b,self.c,self.xp); out=[]
        for k in range(1,self.L1):
            v=self.view(g,*self.l1(k),self.c,self.crossed()); out.append(self.rc(v,v,"x",(g,k-1),to))
        return out
    def ws(self,g):
        to=self.dev(self.a,self.b,self.c,self.xp); out=[]
        for k in range(1,self.L2):
            v=self.line(g,k,self.crossed()); out.append(self.rc(v,v,"w",(g,k-1),to))
        return out
    def cs(self,g):
        v=self.view(g,slice(None),slice(None),self.c,slice(None))
        return [self.rc(v,v,"c",(g,),self.dev(self.a,self.b,1-self.c,self.d))]
    def stage(self,s,g):
        if s==0:
            self.own(g).start()
            for cp in self.zs(g): cp.start()
        elif s==1:
            for cp in self.zs(g): cp.wait_recv()
            self.own(g).wait()
            for cp in self.ys(g)+self.xs(g): cp.start()
        elif s==2:
            for cp in self.ys(g): cp.wait_recv()
            for cp in self.ws(g): cp.start()
        elif s==3:
            for cp in self.xs(g)+self.ws(g): cp.wait_recv()
            for cp in self.cs(g): cp.start()
        else:
            for cp in self.cs(g): cp.wait_recv()
    def tick(self,t):
        for s,o in enumerate(OFFS):
            if isinstance(t,int):
                if 0<=t-o<NC: self.stage(s,jnp.int32(t-o))
            else:
                @pl.when((t-o>=0)&(t-o<NC))
                def _(s=s,o=o): self.stage(s,t-o)
    def finish(self):
        def done(g,_):
            for cp in self.zs(g)+self.ys(g)+self.xs(g)+self.ws(g)+self.cs(g): cp.wait_send()
            return 0
        lax.fori_loop(0,NC,done,0)
    @staticmethod
    def sems(A,B):
        L1,L2=max(A,B),min(A,B); s={"loc":(NC,)}
        for n,k in (("z",L1-1),("y",L2-1),("x",L1-1),("w",L2-1)):
            s[n+"s"]=(NC,k); s[n+"r"]=(NC,k)
        s["cs"]=(NC,); s["cr"]=(NC,)
        return {n:pltpu.SemaphoreType.DMA(v) for n,v in s.items()}

def attn_fwd_head(q8,k,v,klanes,qlanes,h,put):
    l=lane((T,128))
    hm=(l<64) if h==0 else (l>=64)
    qa=jnp.concatenate([jnp.where(hm,q8,jnp.zeros_like(q8)),qlanes],axis=1)
    ka=jnp.concatenate([k,klanes],axis=1)
    tri=lane((QB,QB))<=row((QB,QB))
    for i in range(T//QB):
        n=(i+1)*QB
        s=nt(qa[i*QB:(i+1)*QB],ka[:n])
        sd=jnp.where(tri,s[:,n-QB:],NEG)
        s=jnp.concatenate([s[:,:n-QB],sd],axis=1) if i else sd
        m=jnp.max(s,axis=1,keepdims=True)
        e=jnp.exp(s-m)
        tot=jnp.sum(e,axis=1,keepdims=True)
        put(i,nn(e.astype(BF),v[:n])*(1.0/tot),m+jnp.log(tot))

def forward_kernel(A,B,sem_names,x_ref,og_ref,st_ref,gain_ref,shift_ref,ob_ref,b3_ref,bf_ref,at_ref,uu_ref,wq_ref,wo_ref,wf_ref,wp_ref,
                   u_ref,qkv_out,o_out,lse_ref,r_ref,bo_out,dx2_out,do_out,
                   l_ref,h1_ref,qkv_ref,o_ref,x2_ref,h2_ref,y_ref,dh_ref,kl_ref,ql_ref,wb_ref,wout_ref,bo_ref,do_ref,wsem,osem,*sems):
    G_=Gather(A,B,l_ref,u_ref,dict(zip(sem_names,sems)))
    R=wq_ref.shape[0]
    G_.greet()
    for p in range(8):
        for i in range(3):
            c0=384*p+128*i
            l_ref[c0//1024,:,c0%1024:c0%1024+128]=wq_ref[:,1024*i+128*p:1024*i+128*p+128]
    G_.greeted()
    G_.tick(0); G_.tick(1)
    l_ref[3]=wo_ref[...]
    for j in range(4):
        l_ref[5+2*j]=wp_ref[R*j:R*j+R,:]
    fw=R; S_=D//fw
    half=lane((R,128))<64
    for j in range(4):
        for t in range(8):
            if R==64:
                p0=wf_ref[:,512*t+128*(j//2):512*t+128*(j//2)+128]; p1=wf_ref[:,512*t+256+128*(j//2):512*t+256+128*(j//2)+128]
                ps=[p0,p1]
                f=[x.astype(F32) for x in ps]
                if j%2==0: v=jnp.where(half,f[0],pltpu.roll(f[1],64,1))
                else: v=jnp.where(half,pltpu.roll(f[0],64,1),f[1])
            else:
                f=[wf_ref[:,512*t+128*i:512*t+128*i+128].astype(F32) for i in range(4)]
                ln=lane((R,128)); v=None
                for i in range(4):
                    sh=(32*i-32*j)%128
                    x=pltpu.roll(f[i],sh,1) if sh else f[i]
                    v=x if v is None else jnp.where((ln>=32*i)&(ln<32*i+32),x,v)
            l_ref[4+2*j,:,128*t:128*t+128]=v.astype(BF)
    G_.tick(2)
    def ln0(i,_):
        sl=pl.ds(pl.multiple_of(i*256,256),256)
        c,rs=stats(x_ref[sl,:].astype(F32))
        h1_ref[sl,:]=(c*rs*gain_ref[0:1,:]+shift_ref[0:1,:]).astype(BF)
        r_ref[sl,:]=nt(h1_ref[sl,:],at_ref[...]).astype(BF)
        return 0
    lax.fori_loop(0,2,ln0,0)
    G_.tick(3)
    lax.fori_loop(2,4,ln0,0)
    kl_ref[...]=key_lanes(st_ref[...])
    ql_ref[...]=query_lanes(None)
    lse_ref[...]=jnp.zeros((T,128),F32)
    for t in (4,5,6): G_.tick(t)
    def load(u,slot): return pltpu.make_async_copy(u_ref.at[u],wb_ref.at[slot],wsem.at[slot])
    def w(slot): return wb_ref[slot].reshape(D,D)
    def out(src,dst,k):
        cp=pltpu.make_async_copy(src,dst,osem.at[k]); cp.start(); return cp
    load(0,0).start()
    G_.tick(7)
    t=8
    pend=[]
    wo_cp=pltpu.make_async_copy(u_ref.at[3],wout_ref,wsem.at[4])
    first=(0,2,5,8)
    for u in range(3):
        load(u,u).wait()
        def mix(i,_,u=u):
            sl=pl.ds(pl.multiple_of(i*256,256),256)
            cs=slice(u*1024,u*1024+1024)
            qkv_ref[sl,cs]=(nn(h1_ref[sl,:],w(u))+(nn(r_ref[sl,:],uu_ref[:,cs])+b3_ref[:,cs])).astype(BF)
            return 0
        lax.fori_loop(0,4,mix,0)
        G_.tick(t); t+=1
        if u<2: load(u+1,u+1).start()
        else: wo_cp.start()
        base=t
        def pair(p,_,u=u,base=base):
            qs=pl.ds(pl.multiple_of(p*384,128),128); ks=pl.ds(pl.multiple_of(p*384+128,128),128); vs=pl.ds(pl.multiple_of(p*384+256,128),128)
            oc=pl.ds(pl.multiple_of(p*128,128),128)
            lq=lane((QB,128))
            for h in range(2):
                q8=qkv_ref[:,qs]*jnp.asarray(0.125,BF)
                def put(i,o,ls,h=h):
                    sl=slice(i*QB,(i+1)*QB)
                    if h==0: o_ref[sl,oc]=o.astype(BF)
                    else: o_ref[sl,oc]=jnp.where(lq<64,o_ref[sl,oc],o.astype(BF))
                    lse_ref[sl,:]=jnp.where(lq==2*p+h,ls,lse_ref[sl,:])
                attn_fwd_head(q8,qkv_ref[:,ks],qkv_ref[:,vs],kl_ref[...],ql_ref[...],h,put)
                if h==0 and u==0: G_.tick(base+p-first[u])
            if u>0: G_.tick(base+p-first[u])
            return 0
        lax.fori_loop(first[u],first[u+1],pair,0)
        t=base+first[u+1]-first[u]
    pend.append(out(qkv_ref,qkv_out,0)); pend.append(out(o_ref,o_out,1))
    load(4,0).start(); load(5,1).start()
    wo_cp.wait()
    RB=256
    def mid0(i,_):
        sl=pl.ds(pl.multiple_of(i*RB,RB),RB)
        x2=x_ref[sl,:].astype(F32)+nn(o_ref[sl,:],wout_ref[...].reshape(D,D))+ob_ref[0:1,:]
        x2_ref[sl,:]=x2
        c,rs=stats(x2)
        h2_ref[sl,:]=(c*rs*gain_ref[1:2,:]+shift_ref[1:2,:]).astype(BF)
        y_ref[sl,:]=x2+ob_ref[1:2,:]
        dh_ref[sl,:]=jnp.zeros((RB,D),F32)
        return 0
    lax.fori_loop(0,T//RB,mid0,0)
    G_.tick(t); t+=1
    base=t
    def chunk(j,_):
        s0=2*lax.rem(j,2); s1=s0+1
        load(4+2*j,s0).wait(); load(5+2*j,s1).wait()
        def blk(i,_):
            sl=pl.ds(pl.multiple_of(i*RB,RB),RB)
            wf=wb_ref[s0].reshape(D,D); wp=wb_ref[s1].reshape(D,D)
            f=nn(h2_ref[sl,:],wf)+bf_ref[pl.ds(j,1),:]
            f2=f*f
            th=jnp.tanh(C0*(f+C1*(f2*f)))
            hp=0.5*(1.0+th)
            g=(f*hp).astype(BF)
            gp=hp+(0.5*C0)*f*(1.0-th*th)*(1.0+(3*C1)*f2)
            y_ref[sl,:]+=nn(g,wp)
            dg=nt(og_ref[sl,:],wp)
            df=(dg*gp).astype(BF)
            dh_ref[sl,:]+=nt(df,wf)
            G_.tick(base+4*j+i)
            @pl.when((i==1)&(j<3))
            def _():
                load(6+2*j,2-s0).start(); load(7+2*j,3-s0).start()
            return 0
        lax.fori_loop(0,T//RB,blk,0)
        return 0
    lax.fori_loop(0,4,chunk,0)
    for i in range(T//RB):
        sl=slice(i*RB,(i+1)*RB)
        bo_ref[sl,:]=y_ref[sl,:].astype(BF)
        pend.append(out(bo_ref.at[sl],bo_out.at[sl],2+3*i))
        c,rs=stats(x2_ref[sl,:])
        xh=c*rs
        dy=dh_ref[sl,:]*gain_ref[1:2,:]
        dx2=og_ref[sl,:].astype(F32)+rs*(dy-jnp.mean(dy,axis=-1,keepdims=True)-xh*jnp.mean(dy*xh,axis=-1,keepdims=True))
        x2_ref[sl,:]=dx2
        pend.append(out(x2_ref.at[sl],dx2_out.at[sl],3+3*i))
        do_ref[sl,:]=nt(dx2.astype(BF),wout_ref[...].reshape(D,D)).astype(BF)
        pend.append(out(do_ref.at[sl],do_out.at[sl],4+3*i))
    for cp in pend: cp.wait()
    G_.finish()
def forward_call(A,B,x,og,st,gain,shift,ob,b3,bf4,at,uu,wq,wo,wf,wp):
    R=wq.shape[0]
    sems=Gather.sems(A,B)
    hbm=pl.BlockSpec(memory_space=pl.ANY)
    sd=jax.ShapeDtypeStruct
    return pl.pallas_call(functools.partial(forward_kernel,A,B,list(sems)),
      in_specs=[VM]*14,
      out_specs=[hbm,hbm,hbm,VM,VM,hbm,hbm,hbm],
      out_shape=[sd((NU,A,B,2,R,D),BF),sd((T,3*D),BF),sd((T,D),BF),sd((T,128),F32),sd((T,16),BF),sd((T,D),BF),sd((T,D),F32),sd((T,D),BF)],
      scratch_shapes=[pltpu.VMEM((NU,R,D),BF),pltpu.VMEM((T,D),BF),pltpu.VMEM((T,3*D),BF),pltpu.VMEM((T,D),BF),pltpu.VMEM((T,D),F32),pltpu.VMEM((T,D),BF),
        pltpu.VMEM((T,D),F32),pltpu.VMEM((T,D),F32),pltpu.VMEM((T,128),BF),pltpu.VMEM((T,128),BF),pltpu.VMEM((4,A,B,2,R,D),BF),pltpu.VMEM((A,B,2,R,D),BF),
        pltpu.VMEM((T,D),BF),pltpu.VMEM((T,D),BF),pltpu.SemaphoreType.DMA((5,)),pltpu.SemaphoreType.DMA((14,))]+list(sems.values()),
      compiler_params=pltpu.CompilerParams(collective_id=0,has_side_effects=True,vmem_limit_bytes=60*2**20),name="front")(x,og,st,gain,shift,ob,b3,bf4,at,uu,wq,wo,wf,wp)

def back_kernel(x_ref,gain_ref,shift_ref,st_ref,w_ref,at_ref,uu_ref,r_ref,lse_ref,qkv_ref,do_ref,o_ref,dx2_ref,bo_in,ig_ref,ga_ref,bo_ref,kl_ref,dm_ref):
    p=pl.program_id(0)
    bo_ref[...]=bo_in[...]
    @pl.when(p==0)
    def _():
        kl_ref[...]=key_lanes(st_ref[...])
    l=lane((T,128))
    lse=lse_ref[...]
    lc=[jnp.sum(jnp.where(l==2*p+h,lse,0.0),axis=1,keepdims=True) for h in range(2)]
    def store(kind,sl,val):
        dm_ref[sl,pl.ds(pl.multiple_of(p*384+{"q":0,"k":128,"v":256}[kind],128),128)]=val.astype(BF)
    attn_bwd_pair(qkv_ref[:,0:128],qkv_ref[:,128:256],qkv_ref[:,256:384],do_ref[...],o_ref[...],lc,kl_ref[...],store)
    @pl.when(p==7)
    def _():
        ga_ref[...]=jnp.zeros((4,4,D),F32)
        def blk(i,_):
            sl=pl.ds(pl.multiple_of(i*256,256),256)
            dm=dm_ref[sl,:]
            drb=nt(dm,uu_ref[...]).astype(BF)
            dh=nn(drb,at_ref[...])
            for u in range(3): dh=dh+nt(dm[:,u*1024:u*1024+1024],w_ref[u].reshape(D,D))
            c,rs=stats(x_ref[sl,:].astype(F32))
            xh=c*rs
            h1=(xh*gain_ref[0:1,:]+shift_ref[0:1,:]).astype(BF)
            dy=dh*gain_ref[0:1,:]
            ig_ref[sl,:]=dx2_ref[sl,:]+rs*(dy-jnp.mean(dy,axis=-1,keepdims=True)-xh*jnp.mean(dy*xh,axis=-1,keepdims=True))
            ga=tn(drb,h1)
            gu=tn(r_ref[sl,:],dm)*8.0
            ga_ref[0]+=ga[0:4]
            ga_ref[2]+=ga[8:12]
            for k in range(8):
                ga_ref[1,:,128*k:128*k+128]+=gu[4:8,384*k:384*k+128]
                ga_ref[3,:,128*k:128*k+128]+=gu[12:16,384*k+256:384*k+384]
            return 0
        lax.fori_loop(0,4,blk,0)
def back_call(x,gain,shift,st,u,at,uu,r,lse,qkv,do,o,dx2,bo):
    pb=lambda wd: pl.BlockSpec((T,wd),lambda p:(0,p))
    sd=jax.ShapeDtypeStruct
    ub=pl.BlockSpec((3,)+u.shape[1:],lambda p:(0,)*len(u.shape),pipeline_mode=pl.Buffered(1))
    return pl.pallas_call(back_kernel,grid=(8,),
      in_specs=[VM,VM,VM,VM,ub,VM,VM,VM,VM,pb(384),pb(128),pb(128),VM,pb(128)],
      out_specs=[VM,VM,pb(128)],
      out_shape=[sd((T,D),F32),sd((4,4,D),F32),sd((T,D),BF)],
      scratch_shapes=[pltpu.VMEM((T,128),BF),pltpu.VMEM((T,3*D),BF)],
      compiler_params=pltpu.CompilerParams(vmem_limit_bytes=60*2**20),name="back")(x,gain,shift,st,u,at,uu,r,lse,qkv,do,o,dx2,bo)

def sum_kernel(F,DP,g_ref,o_ref,acc_ref,rcv_ref,ss,rs):
    f=lax.axis_index("fsdp"); d=lax.axis_index("dp")
    partners=[]
    for ax,size,me in (("fsdp",F,f),("dp",DP,d)):
        bit=1
        while bit<size:
            other=me+bit-2*bit*lax.rem(lax.div(me,bit),2)
            partners.append({"fsdp":other,"dp":d} if ax=="fsdp" else {"fsdp":f,"dp":other})
            bit*=2
    bar=pltpu.get_barrier_semaphore()
    for p in partners: pl.semaphore_signal(bar,inc=1,device_id=p,device_id_type=MESH)
    pl.semaphore_wait(bar,len(partners))
    acc_ref[0]=g_ref[...]
    cps=[]
    for s,p in enumerate(partners):
        cp=pltpu.make_async_remote_copy(src_ref=acc_ref.at[s],dst_ref=rcv_ref.at[s],send_sem=ss.at[s],recv_sem=rs.at[s],device_id=p,device_id_type=MESH)
        cp.start(); cps.append(cp)
        cp.wait_recv()
        tot=acc_ref[s]+rcv_ref[s]
        if s+1<len(partners): acc_ref[s+1]=tot
        else: o_ref[...]=tot
    for cp in cps: cp.wait_send()
def sum_call(F,DP,g):
    n=(F.bit_length()-1)+(DP.bit_length()-1)
    return pl.pallas_call(functools.partial(sum_kernel,F,DP),in_specs=[VM],out_specs=VM,out_shape=jax.ShapeDtypeStruct(g.shape,F32),
      scratch_shapes=[pltpu.VMEM((n,)+g.shape,F32),pltpu.VMEM((n,)+g.shape,F32),pltpu.SemaphoreType.DMA((n,)),pltpu.SemaphoreType.DMA((n,))],
      compiler_params=pltpu.CompilerParams(collective_id=1,has_side_effects=True),name="total")(g)

def adapters_prep(ad):
    a=ad.astype(BF).transpose(0,2,1)
    at=jnp.concatenate([a[0],a[0],a[2],a[2]],0)
    u8=(a*jnp.asarray(8,BF)).reshape(4,4,8,1,128)
    z=jnp.zeros((4,8,1,128),BF)
    top=jnp.concatenate([u8[1],z,z],2); low=jnp.concatenate([z,z,u8[3]],2); none=jnp.concatenate([z,z,z],2)
    return at,jnp.concatenate([top,none,low,none],0).reshape(16,3*D)
def solution(mesh):
    F=mesh.shape["fsdp"]; DP=mesh.shape["dp"]
    A,B=(F//4,2) if F<=16 else (2,F//4)
    def per_device(tokens,item_start,og,gains,shifts,wqkv,bqkv,wout,wfc,bfc,wproj,ob,adapters,momentum,average):
        R=wqkv.shape[0]
        b3=bqkv.reshape(3,8,128).transpose(1,0,2).reshape(1,3*D)
        bf4=bfc.reshape(D//R,4,R).transpose(1,0,2).reshape(4,D)
        at,uu=adapters_prep(adapters)
        st=jnp.pad(item_start[::128],(0,120)).reshape(1,128)
        u,qkv,o,lse,r,bo,dx2,do=forward_call(A,B,tokens,og,st,gains,shifts,ob,b3,bf4,at,uu,wqkv,wout,wfc,wproj)
        ig,ga,bo=back_call(tokens,gains,shifts,st,u,at,uu,r,lse,qkv,do,o,dx2,bo)
        grad=sum_call(F,DP,ga).transpose(0,2,1)
        rate=0.01/jnp.sqrt(jnp.float32(tokens.shape[0]*F*DP))
        mom=0.9*momentum+grad
        new=adapters-rate*(grad+0.9*mom)
        avg=0.9*average+0.1*new
        return bo,ig,grad,mom,new,avg,new.astype(BF)
    rows=P(("fsdp","dp"),None); w=P("fsdp",None); n=P()
    return jax.shard_map(per_device,mesh=mesh,
      in_specs=(rows,P(("fsdp","dp")),rows,n,n,w,n,w,w,n,w,n,n,n,n),out_specs=(rows,rows,n,n,n,n,n),check_vma=False)
```

time: 310 us -> 250 us (0.81)
  Pallas kernels: 285 us -> 239 us
  local copies, waits for them, and re-layouts: 19.3 us -> 6.39 us
    pallas_call x4 -> x2, Pallas kernels: 264 us -> 218 us  [the longest x1 158 us: forward_call(): pl.pallas_call(functools.partial(forward_kernel, A, B, list(sems)), in_sp...]
    unnamed x25 -> x9, local copies, waits for them, and re-layouts: 15.9 us -> 1.5 us
where the time goes in v2:
time: 250 us
  Pallas kernels  239 us (96%)
  local copies, waits for them, and re-layouts  6.39 us (3%)
  other arithmetic  3.75 us (2%)
    pallas_call x1, Pallas kernels, forward_call(): pl.pallas_call(functools.partial(forward_kernel, A, B, list(sems)), in_sp...  158 us
    pallas_call x1, Pallas kernels, back_call(): pl.pallas_call(back_kernel, grid=(8,), in_specs=[VM, VM, VM, VM, ub, VM,...  60 us
    pallas_call x1, Pallas kernels, sum_call(): pl.pallas_call(functools.partial(sum_kernel, F, DP), in_specs=[VM], out_s...  20.4 us

profile of v2, /device:TPU:0, one launch (start us, length us, event | category | flops | bytes accessed | tf_op | source)
XLA Modules:
  0.0 249.7 jit_solution(5719378503839984305)
XLA Ops:
  0.6 0.8 slice.19
  1.4 0.5 pad_bitcast_fusion.st_ref
  1.9 0.7 copy.24
  2.6 0.6 reshape.39.b3_ref
  3.3 0.8 reshape.40
  4.1 0.7 reshape.41.bf_ref
  4.8 0.9 broadcast_multiply_fusion
  5.7 0.6 pad_maximum_fusion.at_ref
  6.3 0.1 fusion.4
  6.4 0.7 reshape.42.uu_ref
  7.1 158.3 %front.1 = (bf16[12,4,2,2,64,1024]{5,4,3,2,1,0:T(8,128)(2,1)}, bf16[1024,3072]{1,0:T(8,128)(2,1)}, bf16[1024,1024]{1,0:T(8,128)(2,1)}, f32[1024,128]{1,0:T(8,128...) custom-call(bf16[1024,1024]{1,0:T(8,128)(2,1)} %x_ref.3, ...), custom_call_target="tpu_custom_call" | custom-call | tf_op jit(solution)/shard_map/front/pallas_call | solution.py:327
  165.5 0.0 copy-start.1
  165.5 0.0 copy-start.3
  165.5 0.0 copy-start.2
  165.5 60.0 %back.1 = (f32[1024,1024]{1,0:T(8,128)}, f32[4,4,1024]{2,1,0:T(4,128)}, bf16[1024,1024]{1,0:T(8,128)(2,1)}) custom-call(bf16[1024,1024]{1,0:T(8,128)(2,1)} %x_ref.3, f32[2,1024]{1,0:T(2,128)} %gain_ref.3, f32[2,1024]{1,0:T(2,128)} %shift_ref.3, s32[1,128]{1,0:T(1,128)} %pad_bitcast_fusion.st_ref, bf16[12,4,2,2,64,1024]{5,4,3,2,1,0:T(8,128)(2,1)} %get-tuple-element.18.w_ref, ...), custom_call_target="tpu_custom_call" | custom-call | tf_op jit(solution)/shard_map/back/pallas_call | solution.py:375
  225.5 20.4 %total.1 = f32[4,4,1024]{2,1,0:T(4,128)} custom-call(f32[4,4,1024]{2,1,0:T(4,128)} %get-tuple-element.28.g_ref), custom_call_target="tpu_custom_call" | custom-call | tf_op jit(solution)/shard_map/total/pallas_call | solution.py:406
  246.0 0.0 copy-done.1
  246.0 0.0 copy-done.3
  246.0 1.5 fusion.6
  247.5 0.0 copy-start
  247.5 0.0 copy-done.2
  247.5 0.7 multiply_add_fusion
  248.2 1.5 copy.29
  249.7 0.0 copy-done
  (6 shorter events, 0.1 us)
Async XLA Ops:
  165.5 80.5 %copy-start.1 = (f32[4,1024,4]{1,2,0:T(4,128)S(1)}, f32[4,1024,4]{1,2,0:T(4,128)}, u32[]{:S(2)}) copy-start(f32[4,1024,4]{1,2,0:T(4,128)} %param.27) | copy-start | bytes 196612
  165.5 80.5 %copy-start.3 = (f32[4,1024,4]{1,2,0:T(4,128)S(1)}, f32[4,1024,4]{1,2,0:T(4,128)}, u32[]{:S(2)}) copy-start(f32[4,1024,4]{1,2,0:T(4,128)} %param.28) | copy-start | bytes 196612
  165.5 82.0 %copy-start.2 = (f32[4,1024,4]{1,2,0:T(4,128)S(1)}, f32[4,1024,4]{1,2,0:T(4,128)}, u32[]{:S(2)}) copy-start(f32[4,1024,4]{1,2,0:T(4,128)} %param.29) | copy-start | bytes 196612
  247.5 2.1 copy-start
